TPU v7x, 32 devices: a whole 2x2x4 slice. The times are simulated.
32 devices in a mesh: grp: 2 (over x), ex: 8 (over z, y), lay: 2 (over core).
Axes of the slice: x: 2, y: 2, z: 4, core: 2. Of those that a mesh axis runs over, the one named last changes fastest.
Arguments:
- queries: bfloat16 [512, 2, 4096], P('ex', 'lay'), may hold values from -4 to 4
- basis_s: float32 [2, 64, 64], P('lay'), may hold values from -1 to 1, as said below
- basis_a: float32 [2, 64, 64], P('lay'), may hold values from -1 to 1, as said below
- eigvals: float32 [2, 64, 64], P('lay'), may hold values from 0.004 to 20, as said below
- train_grads: bfloat16 [16384, 2, 4096], P(('grp', 'ex'), 'lay'), parts along dimension 0, may hold values from -0.0625 to 0.0625
- example_ids: int32 [16, 1024], P(('grp', 'ex')), parts along dimension 0, may hold values from 0 to 1023, each once within a row
Outputs:
- scores: float32 [512, 16384], P(None, ('grp', 'ex', 'lay')), parts along dimension 1
There are 2 independent parts, one for each index of `grp`. A program takes and returns all parts, laid end to end along the dimension named above; an argument that names none is the same for every part. Nothing has to cross between parts.
Inputs may be any that keep to these rules, and one draw needn't show every extreme that they name: `basis_s`: each layer's basis has orthonormal columns. `basis_a`: each layer's basis has orthonormal columns. `eigvals`: positive.
All inputs are finite; a program needn't handle non-finite values.
Results may differ from a plain program's by a relative error of at most 0.0029.
Values may be sent and summed in bfloat16 or wider, within the bound.
A program may use at most 64 MiB of HBM per device.

v0:
```python
import functools

import jax
import jax.numpy as jnp
from jax import lax
from jax.experimental import pallas as pl
from jax.experimental.pallas import tpu as pltpu
from jax.sharding import PartitionSpec as P

damp_ratio = 0.1
pairs = 4
shared = 2
MESH = pl.DeviceIdType.MESH


def precondition(grads, basis_s, basis_a, eigvals):
    number_rows = grads.shape[0]
    layer_count = grads.shape[1]
    rank = basis_s.shape[-1]
    high = lax.Precision.HIGH
    expanded = grads.astype(jnp.float32).reshape(number_rows, layer_count, rank, rank)
    half_turn = jnp.einsum("nlik,lkm->nlim", expanded, basis_a, precision=high)
    rotated = jnp.einsum("lij,nlim->nljm", basis_s, half_turn, precision=high)
    damping = damp_ratio * jnp.mean(eigvals, axis=(1, 2), keepdims=True)
    scaled = rotated / (eigvals + damping)[None]
    turned_back = jnp.einsum("nljm,lpm->nljp", scaled, basis_a, precision=high)
    restored = jnp.einsum("lij,nljp->nlip", basis_s, turned_back, precision=high)
    return restored.reshape(number_rows, layer_count, rank * rank).astype(jnp.bfloat16)


def score_kernel(
    line, own_ref, ids_ref, train_ref, out_ref,
    stored, hot, perm, held, acc, arrived,
    load_sem, own_sem, z_recv, zr_send, zl_send, y_recv, y_send, x_recv, x_send, twin_recv, twin_send,
    c_recv, c_send,
):
    grp = lax.axis_index("grp")
    ex = lax.axis_index("ex")
    core = lax.axis_index("lay")
    zz = ex // 2
    w = ex % 2
    side = grp % 2
    rows = own_ref.shape[2]
    examples = train_ref.shape[0]
    chunk = own_ref.shape[3]
    half = examples // 2
    right = {"ex": lax.rem(ex + 2, 2 * line)}
    left = {"ex": lax.rem(ex + 2 * line - 2, 2 * line)}
    across_y = {"ex": zz * 2 + (1 - w)}
    across_x = {"grp": (grp // 2) * 2 + (1 - side)}
    across_c = {"lay": 1 - core}
    has_left = zz > 0
    has_right = zz < line - 1

    def load(p):
        return pltpu.make_async_copy(
            train_ref.at[:, pl.ds(p * 2 * chunk, 2 * chunk)], stored.at[p], load_sem.at[p]
        )

    def pick(p, first, second):
        @pl.when(p < shared)
        def _():
            first()

        @pl.when(p >= shared)
        def _():
            second()

    def z_copy(src, b, p, which, send, target):
        return pltpu.make_async_remote_copy(
            src_ref=src, dst_ref=held.at[b, p, which, w], send_sem=send.at[b, p],
            recv_sem=z_recv.at[b, p], device_id=target, device_id_type=MESH,
        )

    def own_z(p, send, target):
        pick(
            p,
            lambda: z_copy(own_ref.at[p, side], zz, p, side, send, target).start(),
            lambda: z_copy(own_ref.at[p], zz, p, slice(None), send, target).start(),
        )

    def pass_z(b, p, send, target, act):
        pick(
            p,
            lambda: act(z_copy(held.at[b, p, side, w], b, p, side, send, target)),
            lambda: act(z_copy(held.at[b, p, :, w], b, p, slice(None), send, target)),
        )

    def begin(copy):
        copy.start()

    def landed(copy):
        copy.wait_recv()

    def left_here(copy):
        copy.wait_send()

    def y_copy(src, b, p):
        return pltpu.make_async_remote_copy(
            src_ref=src, dst_ref=held.at[b, p, side, w], send_sem=y_send.at[b, p],
            recv_sem=y_recv.at[b, p], device_id=across_y, device_id_type=MESH,
        )

    def y_whole(b, p, column):
        slot = held.at[b, p, :, column]
        return pltpu.make_async_remote_copy(
            src_ref=slot, dst_ref=slot, send_sem=y_send.at[b, p],
            recv_sem=y_recv.at[b, p], device_id=across_y, device_id_type=MESH,
        )

    def twin_copy(b, p, which):
        slot = held.at[b, p, which, w]
        return pltpu.make_async_remote_copy(
            src_ref=slot, dst_ref=slot, send_sem=twin_send.at[b, p],
            recv_sem=twin_recv.at[b, p], device_id=across_x, device_id_type=MESH,
        )

    def whole_over_y(t, p):
        return jnp.logical_and(jnp.asarray(t) != 0, jnp.asarray(p) == pairs - 1)

    def from_twin(t, p):
        return jnp.logical_and(jnp.asarray(t) != 0, jnp.asarray(p) < shared)

    def y_arrival(b, p):
        slot = held.at[b, p, side, 1 - w]
        return pltpu.make_async_remote_copy(
            src_ref=slot, dst_ref=slot, send_sem=y_send.at[b, p],
            recv_sem=y_recv.at[b, p], device_id=across_y, device_id_type=MESH,
        )

    def x_copy(b, p, which):
        slot = held.at[b, p, which, 1 - w]
        return pltpu.make_async_remote_copy(
            src_ref=slot, dst_ref=slot, send_sem=x_send.at[b, p],
            recv_sem=x_recv.at[b, p], device_id=across_x, device_id_type=MESH,
        )

    def c_copy(b):
        return pltpu.make_async_remote_copy(
            src_ref=acc.at[b, 1 - core], dst_ref=arrived.at[b], send_sem=c_send.at[b],
            recv_sem=c_recv.at[b], device_id=across_c, device_id_type=MESH,
        )

    @pl.loop(0, pairs)
    def _(p):
        load(p).start()

    barrier = pltpu.get_barrier_semaphore()

    @pl.when(has_left)
    def _():
        pl.semaphore_signal(barrier, inc=1, device_id=left, device_id_type=MESH)

    @pl.when(has_right)
    def _():
        pl.semaphore_signal(barrier, inc=1, device_id=right, device_id_type=MESH)

    for target in (across_y, across_x, across_c):
        pl.semaphore_signal(barrier, inc=1, device_id=target, device_id_type=MESH)
    pl.semaphore_wait(barrier, 3 + has_left.astype(jnp.int32) + has_right.astype(jnp.int32))

    @pl.loop(0, pairs)
    def _(p):
        @pl.when(has_right)
        def _():
            own_z(p, zr_send, right)

        @pl.when(has_left)
        def _():
            own_z(p, zl_send, left)

        y_copy(own_ref.at[p, side], zz, p).start()

    @pl.loop(0, pairs)
    def _(p):
        pltpu.make_async_copy(own_ref.at[p], held.at[zz, p, :, w], own_sem.at[p]).start()

    spread = jnp.broadcast_to(ids_ref[...].astype(jnp.float32), (128, examples)).T
    lanes = lax.broadcasted_iota(jnp.int32, (examples, 128), 1).astype(jnp.float32)
    for tile in range(examples // 128):
        hot[:, tile * 128:(tile + 1) * 128] = jnp.where(
            spread == lanes + float(tile * 128), 1.0, 0.0
        ).astype(jnp.bfloat16)

    @pl.loop(0, pairs)
    def _(p):
        pltpu.make_async_copy(own_ref.at[p], held.at[zz, p, :, w], own_sem.at[p]).wait()

    def both(s, act):
        t = s // pairs
        p = s % pairs
        valid = jnp.logical_and(jnp.asarray(s) >= 0, jnp.asarray(t) < line)

        @pl.when(jnp.logical_and(valid, zz - t >= 0))
        def _():
            act(zz - t, t, p, True)

        @pl.when(jnp.logical_and(jnp.logical_and(valid, jnp.asarray(t) > 0), zz + t < line))
        def _():
            act(zz + t, t, p, False)

    def relay_z(b, t, p, from_left):
        @pl.when(t > 0)
        def _():
            if from_left:
                pass_z(b, p, zr_send, left, landed)

                @pl.when(has_right)
                def _():
                    pass_z(b, p, zr_send, right, begin)
            else:
                pass_z(b, p, zl_send, right, landed)

                @pl.when(has_left)
                def _():
                    pass_z(b, p, zl_send, left, begin)

            @pl.when(p < shared)
            def _():
                twin_copy(b, p, side).start()

            @pl.when(p < pairs - 1)
            def _():
                y_copy(held.at[b, p, side, w], b, p).start()

            @pl.when(p == pairs - 1)
            def _():
                y_whole(b, p, w).start()

    def relay_x(b, t, p, from_left):
        @pl.when(jnp.logical_not(whole_over_y(t, p)))
        def _():
            y_arrival(b, p).wait_recv()
            x_copy(b, p, side).start()

    def multiply(b, t, p, from_left):
        @pl.when(from_twin(t, p))
        def _():
            twin_copy(b, p, 1 - side).wait_recv()

        @pl.when(whole_over_y(t, p))
        def _():
            y_whole(b, p, 1 - w).wait_recv()

        @pl.when(jnp.logical_not(whole_over_y(t, p)))
        def _():
            x_copy(b, p, 1 - side).wait_recv()

        for part in range(2):
            value = None
            for h in range(2):
                term = lax.dot_general(
                    held[b, p, h].reshape(2 * rows, chunk),
                    perm[p, h, part * half:(part + 1) * half, :],
                    (((1,), (1,)), ((), ())), preferred_element_type=jnp.float32,
                )
                value = term if value is None else value + term

            @pl.when(p == 0)
            def _():
                acc[b, part] = value

            @pl.when(p > 0)
            def _():
                acc[b, part] = acc[b, part] + value

        @pl.when(p == pairs - 1)
        def _():
            c_copy(b).start()

    def finish(b, t, p, from_left):
        @pl.when(p == pairs - 1)
        def _():
            c_copy(b).wait_recv()
            out_ref[b] = acc[b, core] + arrived[b]

    @pl.loop(0, pairs)
    def _(p):
        relay_x(zz, 0, p, True)

    def reached(s):
        ready = jnp.minimum(2 * (s - pairs + 1), s + pairs - 1)
        return jnp.minimum(jnp.maximum(ready, 0), line * pairs)

    @pl.loop(0, (line + 1) * pairs)
    def _(s):
        both(s + pairs, relay_z)

        @pl.when(s > 0)
        def _():
            both(s + pairs - 1, relay_x)

        @pl.when(s < pairs)
        def _():
            load(s).wait()

            @pl.loop(0, 4)
            def _(part):
                quarter = examples // 4
                picked = pl.ds(part * quarter, quarter)
                for h in range(2):
                    perm[s, h, picked, :] = jnp.dot(
                        hot[picked, :], stored[s, :, h * chunk:(h + 1) * chunk],
                        preferred_element_type=jnp.float32,
                    ).astype(jnp.bfloat16)

        @pl.loop(reached(s - 1), reached(s))
        def _(m):
            both(m, multiply)
            both(m - 1, finish)

    both(line * pairs - 1, finish)

    @pl.loop(0, line * pairs)
    def _(s):
        b = s // pairs
        p = s % pairs

        @pl.when(jnp.logical_and(has_right, b <= zz))
        def _():
            pass_z(b, p, zr_send, right, left_here)

        @pl.when(jnp.logical_and(has_left, b >= zz))
        def _():
            pass_z(b, p, zl_send, left, left_here)

        t = b - zz

        @pl.when(from_twin(t, p))
        def _():
            twin_copy(b, p, side).wait_send()

        @pl.when(whole_over_y(t, p))
        def _():
            y_whole(b, p, w).wait_send()

        @pl.when(jnp.logical_not(whole_over_y(t, p)))
        def _():
            y_copy(held.at[b, p, side, w], b, p).wait_send()
            x_copy(b, p, side).wait_send()

        @pl.when(p == 0)
        def _():
            c_copy(b).wait_send()


def scores_of(own, ids, train, devices):
    rows = own.shape[2]
    chunk = own.shape[3]
    examples = train.shape[0]
    line = devices // 2
    dma = pltpu.SemaphoreType.DMA
    grid_sems = [dma((line, pairs)) for _ in range(9)]
    return pl.pallas_call(
        functools.partial(score_kernel, line),
        out_shape=jax.ShapeDtypeStruct((line, 2 * rows, examples // 2), jnp.float32),
        in_specs=[
            pl.BlockSpec(memory_space=pltpu.VMEM),
            pl.BlockSpec(memory_space=pltpu.VMEM),
            pl.BlockSpec(memory_space=pl.ANY),
        ],
        out_specs=pl.BlockSpec(memory_space=pltpu.VMEM),
        scratch_shapes=[
            pltpu.VMEM((pairs, examples, 2 * chunk), jnp.bfloat16),
            pltpu.VMEM((examples, examples), jnp.bfloat16),
            pltpu.VMEM((pairs, 2, examples, chunk), jnp.bfloat16),
            pltpu.VMEM((line, pairs, 2, 2, rows, chunk), jnp.bfloat16),
            pltpu.VMEM((line, 2, 2 * rows, examples // 2), jnp.float32),
            pltpu.VMEM((line, 2 * rows, examples // 2), jnp.float32),
            dma((pairs,)),
            dma((pairs,)),
            *grid_sems,
            dma((line,)),
            dma((line,)),
        ],
        compiler_params=pltpu.CompilerParams(
            collective_id=0, has_side_effects=True, vmem_limit_bytes=56 * 1024 * 1024
        ),
    )(own, ids, train)


def shards(devices, queries, basis_s, basis_a, eigvals, train_grads, example_ids):
    stored = train_grads.reshape(train_grads.shape[0], -1)
    own_rows = precondition(queries, basis_s, basis_a, eigvals)
    rows = own_rows.shape[0]
    cut = own_rows.reshape(rows, 2 * pairs, -1).transpose(1, 0, 2)
    cut = cut.reshape(pairs, 2, rows, cut.shape[-1])
    scores = scores_of(cut, example_ids, stored, devices)
    return scores.reshape(devices * rows, -1)


def solution(mesh):
    return jax.shard_map(
        functools.partial(shards, mesh.shape["ex"]),
        mesh=mesh,
        in_specs=(
            P("ex", "lay", None),
            P("lay", None, None),
            P("lay", None, None),
            P("lay", None, None),
            P(("grp", "ex"), "lay", None),
            P(("grp", "ex"), None),
        ),
        out_specs=P(None, ("grp", "ex", "lay")),
        check_vma=False,
    )
```

profile of v0, /device:TPU:1, one launch (start us, length us, event | category | flops | bytes accessed | tf_op | source)
XLA Modules:
  0.0 68.3 jit_solution(11871206492707159020)
XLA Ops:
  0.0 0.0 copy-start
  0.0 1.4 %reduce_sum.9 = f32[]{:T(128)} reduce(f32[1,64,64]{2,1,0:T(8,128)} %param.9, f32[]{:T(128)} %constant.6.clone.1), dimensions={0,1,2}, to_apply=%region_0.0 | reduce | flops 4095 | bytes 16392 | tf_op jit(solution)/shard_map/reduce_sum | solution.py:24
  2.0 0.8 %add_bitcast_fusion = f32[64,64]{1,0:T(8,128)S(1)} fusion(f32[1,64,64]{2,1,0:T(8,128)} %param.9, f32[]{:T(128)S(6)} %mul.4), kind=kLoop, calls=%fused_computation.13 | loop fusion | flops 4096 | bytes 32772 | tf_op jit(solution)/shard_map/div | solution.py:25
  2.8 0.1 copy.10
  2.9 0.0 copy-start.1
  2.9 2.1 %reshape.52 = bf16[64,64,64]{2,1,0:T(8,128)(2,1)S(1)} reshape(bf16[64,1,4096]{2,0,1:T(8,128)(2,1)} %param.6) | data formatting | bytes 1048576 | tf_op jit(solution)/shard_map/reshape.1
  5.0 0.0 copy-done
  5.0 2.1 %fusion.8 = f32[64,64,64]{2,0,1:T(8,128)S(1)} fusion(bf16[64,64,64]{2,1,0:T(8,128)(2,1)S(1)} %reshape.52, f32[1,64,64]{2,1,0:T(8,128)S(1)} %copy-done), kind=kOutput, calls=%fused_computation.9 | convolution fusion | flops 100663296 | bytes 1589248 | tf_op jit(solution)/shard_map/nlik,lkm->nlim/dot_general | solution.py:22
  7.1 0.0 copy-done.1
  7.1 1.0 %fusion.3 = f32[64,64,64]{2,1,0:T(8,128)S(1)} fusion(f32[64,64,64]{2,0,1:T(8,128)S(1)} %fusion.8, f32[1,64,64]{2,1,0:T(8,128)S(1)} %copy-done.1), kind=kOutput, calls=%fused_computation.3 | convolution fusion | flops 100663296 | bytes 2113536 | tf_op jit(solution)/shard_map/lij,nlim->nljm/dot_general | solution.py:23
  8.1 1.0 %fusion.1 = f32[64,64,64]{1,2,0:T(8,128)S(1)} fusion(f32[64,64,64]{2,1,0:T(8,128)S(1)} %fusion.3, f32[64,64]{0,1:T(8,128)S(1)} %copy.10, f32[1,64,64]{2,1,0:T(8,128)S(1)} %copy-done), kind=kOutput, calls=%fused_computation.2 | convolution fusion | flops 100925440 | bytes 2129920 | tf_op jit(solution)/shard_map/nljm,lpm->nljp/dot_general | solution.py:26
  9.1 1.0 %fusion.5 = bf16[64,1,64,64]{2,3,0,1:T(8,128)(2,1)S(1)} fusion(f32[64,64,64]{1,2,0:T(8,128)S(1)} %fusion.1, f32[1,64,64]{2,1,0:T(8,128)S(1)} %copy-done.1), kind=kOutput, calls=%fused_computation.6 | convolution fusion | flops 100925440 | bytes 1589248 | tf_op jit(solution)/shard_map/lij,nljp->nlip/dot_general | solution.py:27
  10.1 0.7 copy.11
  10.8 0.6 convert_element_type.19
  11.4 0.9 %copy.12 = bf16[8,64,512]{2,1,0:T(8,128)(2,1)} copy(bf16[8,64,512]{2,0,1:T(8,128)(2,1)S(1)} %bitcast.51) | data formatting | bytes 1048576 | tf_op jit(solution)/shard_map/transpose | solution.py:386
  12.3 53.7 %shard_map.64 = f32[4,128,512]{2,1,0:T(8,128)} custom-call(bf16[4,2,64,512]{3,2,1,0:T(8,128)(2,1)} %bitcast.52, s32[1,1024]{1,0:T(1,128)} %ids_ref.1, bf16[1024,4096]{1,0:T(8,128)(2,1)} %bitcast.49), custom_call_target="tpu_custom_call" | custom-call | tf_op jit(solution)/shard_map/pallas_call | solution.py:354
  66.1 2.3 %copy.16 = f32[512,512]{1,0:T(8,128)} copy(f32[512,512]{1,0:T(8,128)} %bitcast.50) | data formatting | bytes 2097152
Async XLA Ops:
  0.0 5.0 %copy-start = (f32[1,64,64]{2,1,0:T(8,128)S(1)}, f32[1,64,64]{2,1,0:T(8,128)}, u32[]{:S(2)}) copy-start(f32[1,64,64]{2,1,0:T(8,128)} %param.8) | copy-start | bytes 49156
  2.9 4.2 %copy-start.1 = (f32[1,64,64]{2,1,0:T(8,128)S(1)}, f32[1,64,64]{2,1,0:T(8,128)}, u32[]{:S(2)}) copy-start(f32[1,64,64]{2,1,0:T(8,128)} %param.7) | copy-start | bytes 49156
where the time goes:
time: 68.6 us; the launch traced here: 68.3 us
  Pallas kernels  53.7 us (78%)
  local copies, waits for them, and re-layouts  6.63 us (10%)
  matrix products  5.1 us (7%)
  other arithmetic  2.14 us (3%)
  between operations  0.73 us (1%)
    pallas_call x1, Pallas kernels, scores_of(): pl.pallas_call(functools.partial(score_kernel, line), out_shape=jax.Shape...  53.7 us
    unnamed x5, local copies, waits for them, and re-layouts  2.27 us
    dot_general x1, matrix products, precondition(): half_turn = jnp.einsum('nlik,lkm->nlim', expanded, basis_a, precision=high)  2.15 us
    another operation x1, local copies, waits for them, and re-layouts  2.07 us
    reduce_sum x1, other arithmetic, precondition(): damping = damp_ratio * jnp.mean(eigvals, axis=(1, 2), keepdims=True)  1.38 us

commit v1 on v0

v1 whole, which is shorter than its diff:
```python
import functools

import jax
import jax.numpy as jnp
from jax import lax
from jax.experimental import pallas as pl
from jax.experimental.pallas import tpu as pltpu
from jax.sharding import PartitionSpec as P

damp_ratio = 0.1
chunks = 8
loads = 4
window = 256
MESH = pl.DeviceIdType.MESH


def precondition(grads, basis_s, basis_a, eigvals):
    number_rows = grads.shape[0]
    layer_count = grads.shape[1]
    rank = basis_s.shape[-1]
    high = lax.Precision.HIGH
    expanded = grads.astype(jnp.float32).reshape(number_rows, layer_count, rank, rank)
    half_turn = jnp.einsum("nlik,lkm->nlim", expanded, basis_a, precision=high)
    rotated = jnp.einsum("lij,nlim->nljm", basis_s, half_turn, precision=high)
    damping = damp_ratio * jnp.mean(eigvals, axis=(1, 2), keepdims=True)
    scaled = rotated / (eigvals + damping)[None]
    turned_back = jnp.einsum("nljm,lpm->nljp", scaled, basis_a, precision=high)
    restored = jnp.einsum("lij,nljp->nlip", basis_s, turned_back, precision=high)
    return restored.reshape(number_rows, layer_count, rank * rank).astype(jnp.bfloat16)


def score_kernel(
    line, own_ref, ids_ref, train_ref, out_ref,
    stored, hot, perm, held, acc, arrived, total,
    load_sem, own_sem, z_recv, y_recv, x_recv, zr_send, zl_send, y_send, x_send, c_recv, c_send, out_sem,
):
    grp = lax.axis_index("grp")
    ex = lax.axis_index("ex")
    core = lax.axis_index("lay")
    zz = ex // 2
    w = ex % 2
    side = grp % 2
    rows = own_ref.shape[1]
    examples = train_ref.shape[0]
    chunk = own_ref.shape[2]
    half = examples // 2
    wide = train_ref.shape[1] // loads
    per_load = chunks // loads
    right = {"ex": lax.rem(ex + 2, 2 * line)}
    left = {"ex": lax.rem(ex + 2 * line - 2, 2 * line)}
    across_y = {"ex": zz * 2 + (1 - w)}
    across_x = {"grp": (grp // 2) * 2 + (1 - side)}
    across_c = {"lay": 1 - core}
    has_left = zz > 0
    has_right = zz < line - 1
    lefts = zz
    rights = line - 1 - zz
    both_ways = jnp.minimum(lefts, rights)

    def z_chunk(k):
        return jnp.where(
            k < 2, 2 * side + k, jnp.where(k == 2, 4 + side, jnp.where(k < 5, 3 + k, 5 - side))
        )

    def own_chunk(k):
        return jnp.where(k < 2, 2 * side + k, jnp.where(k == 2, 4 + side, 6 + side))

    def remote(src, dst, send, recv, target):
        return pltpu.make_async_remote_copy(
            src_ref=src, dst_ref=dst, send_sem=send, recv_sem=recv,
            device_id=target, device_id_type=MESH,
        )

    def load(p):
        return pltpu.make_async_copy(
            train_ref.at[:, pl.ds(p * wide, wide)], stored.at[p], load_sem.at[p]
        )

    def z_copy(b, k, send, target):
        slot = held.at[b, z_chunk(k), w]
        return remote(slot, slot, send.at[b], z_recv.at[b, k], target)

    def y_copy(b, k, c, column):
        slot = held.at[b, c, column]
        return remote(slot, slot, y_send.at[b], y_recv.at[b, k], across_y)

    def x_copy(b, k, c, column):
        slot = held.at[b, c, column]
        return remote(slot, slot, x_send.at[b], x_recv.at[b, k], across_x)

    def c_copy(b):
        return remote(acc.at[b, 1 - core], arrived.at[b], c_send.at[b], c_recv.at[b], across_c)

    def out_copy(b):
        return pltpu.make_async_copy(total.at[b], out_ref.at[b], out_sem.at[b])

    def block_of(j):
        i = j - 1
        paired = i < 2 * both_ways
        t = jnp.where(paired, i // 2 + 1, j - both_ways)
        from_left = jnp.where(paired, jnp.asarray(i % 2 == 0).astype(jnp.int32), (lefts > rights).astype(jnp.int32))
        return jnp.where(from_left > 0, zz - t, zz + t)

    @pl.loop(0, loads)
    def _(p):
        load(p).start()

    barrier = pltpu.get_barrier_semaphore()

    @pl.when(has_left)
    def _():
        pl.semaphore_signal(barrier, inc=1, device_id=left, device_id_type=MESH)

    @pl.when(has_right)
    def _():
        pl.semaphore_signal(barrier, inc=1, device_id=right, device_id_type=MESH)

    for target in (across_y, across_x, across_c):
        pl.semaphore_signal(barrier, inc=1, device_id=target, device_id_type=MESH)

    own = pltpu.make_async_copy(own_ref, held.at[zz, :, w], own_sem)
    own.start()
    own.wait()
    pl.semaphore_wait(barrier, 3 + has_left.astype(jnp.int32) + has_right.astype(jnp.int32))

    @pl.loop(0, 6)
    def _(k):
        @pl.when(has_right)
        def _():
            z_copy(zz, k, zr_send, right).start()

        @pl.when(has_left)
        def _():
            z_copy(zz, k, zl_send, left).start()

        @pl.when(k < 4)
        def _():
            y_copy(zz, k, own_chunk(k), w).start()

    spread = jnp.broadcast_to(ids_ref[...].astype(jnp.float32), (128, examples)).T
    lanes = lax.broadcasted_iota(jnp.int32, (examples, 128), 1).astype(jnp.float32)
    for tile in range(examples // 128):
        hot[:, tile * 128:(tile + 1) * 128] = jnp.where(
            spread == lanes + float(tile * 128), 1.0, 0.0
        ).astype(jnp.bfloat16)

    def z_arrival(b, k, from_left):
        z_copy(b, k, zr_send, right).wait_recv()
        if from_left:
            @pl.when(has_right)
            def _():
                z_copy(b, k, zr_send, right).start()
        else:
            @pl.when(has_left)
            def _():
                z_copy(b, k, zl_send, left).start()

        @pl.when(k < 5)
        def _():
            y_copy(b, k, z_chunk(k), w).start()

        @pl.when(k < 2)
        def _():
            x_copy(b, k, z_chunk(k), w).start()

    def relay(tick):
        t = tick // 6 + 1
        k = tick % 6

        @pl.when(jnp.logical_and(t < line, zz - t >= 0))
        def _():
            z_arrival(zz - t, k, True)

        @pl.when(jnp.logical_and(t < line, zz + t < line))
        def _():
            z_arrival(zz + t, k, False)

        q = tick - 1

        @pl.when(jnp.logical_and(q >= 0, q < 4))
        def _():
            y_copy(zz, q, own_chunk(q), 1 - w).wait_recv()
            x_copy(zz, q, own_chunk(q), 1 - w).start()

        @pl.when(jnp.logical_and(q >= 4, q < 4 + 5 * (line - 1)))
        def _():
            b = block_of((q - 4) // 5 + 1)
            k = (q - 4) % 5
            y_copy(b, k, z_chunk(k), 1 - w).wait_recv()

            @pl.when(k < 3)
            def _():
                x_copy(b, k + 2, z_chunk(k), 1 - w).start()

    def permute(c):
        p = c // per_load
        at = c % per_load

        @pl.when(at == 0)
        def _():
            load(p).wait()

        columns = pl.ds(pl.multiple_of(at * chunk, chunk), chunk)

        @pl.loop(0, 4)
        def _(part):
            quarter = examples // 4
            picked = pl.ds(part * quarter, quarter)
            perm[c, picked, :] = jnp.dot(
                hot[picked, :], stored[p, :, columns], preferred_element_type=jnp.float32
            ).astype(jnp.bfloat16)

    per_half = half // window

    def terms(b, n, picked):
        part = pl.ds(pl.multiple_of(n * window, window), window)
        value = None
        for c in picked:
            term = lax.dot_general(
                held[b, c].reshape(2 * rows, chunk), perm[c, part, :],
                (((1,), (1,)), ((), ())), preferred_element_type=jnp.float32,
            )
            value = term if value is None else value + term
        return value

    def columns_of(n):
        return n // per_half, pl.ds(pl.multiple_of((n % per_half) * window, window), window)

    def whole_block(b, n):
        h, at = columns_of(n)
        acc[b, h, :, at] = terms(b, n, range(chunks))

    def x_arrivals(b, first, last):
        for k in range(first, last):
            x_copy(b, k, 0, w).wait_recv()

    def finish(b):
        c_copy(b).wait_recv()
        total[b] = acc[b, core] + arrived[b]
        out_copy(b).start()

    tiles = examples // window
    first_own = 8

    def compute(tick):
        @pl.when(tick < chunks)
        def _():
            permute(tick)

        for at in range(2):
            @pl.when(tick == first_own + at)
            def _():
                if at == 0:
                    x_arrivals(zz, 0, 4)

                @pl.loop(at * (tiles // 2), (at + 1) * (tiles // 2))
                def _(n):
                    whole_block(zz, n)

                if at == 1:
                    c_copy(zz).start()

            j = (tick - 6 - at) // 6

            @pl.when(jnp.logical_and(tick % 6 == at, jnp.logical_and(tick >= 12, j < line - 1)))
            def _():
                b = block_of(j)
                if at == 0:
                    x_arrivals(b, 0, 5)

                @pl.loop(at * (tiles // 2), (at + 1) * (tiles // 2))
                def _(n):
                    whole_block(b, n)

                if at == 1:
                    c_copy(b).start()

    ticks = max(6 * (line - 1), 5 * line, 6 * (line - 2) + 8)

    @pl.loop(0, ticks)
    def _(tick):
        relay(tick)
        compute(tick)

    last = block_of(line - 1)
    mine = (2 * side, 2 * side + 1, 4 + side, 6, 7)
    pair = (2 - 2 * side, 3 - 2 * side)
    single = (5 - side,)

    @pl.loop(0, tiles)
    def _(n):
        h, at = columns_of(n)
        acc[last, h, :, at] = terms(last, n, mine)

    @pl.loop(0, line)
    def _(b):
        @pl.when(b != last)
        def _():
            finish(b)

    x_arrivals(last, 0, 4)

    @pl.loop(0, tiles)
    def _(n):
        h, at = columns_of(n)
        acc[last, h, :, at] = acc[last, h, :, at] + terms(last, n, pair)

    x_arrivals(last, 4, 5)

    @pl.loop(0, tiles)
    def _(n):
        h, at = columns_of(n)
        acc[last, h, :, at] = acc[last, h, :, at] + terms(last, n, single)

    c_copy(last).start()
    finish(last)

    def sent(b, count, send):
        span = held.at[b, pl.ds(0, count), w]
        remote(span, span, send.at[b], z_recv.at[b, 0], across_y).wait_send()

    @pl.loop(0, line)
    def _(b):
        @pl.when(jnp.logical_and(has_right, b <= zz))
        def _():
            sent(b, 6, zr_send)

        @pl.when(jnp.logical_and(has_left, b >= zz))
        def _():
            sent(b, 6, zl_send)

        @pl.when(b == zz)
        def _():
            sent(b, 4, y_send)
            sent(b, 4, x_send)

        @pl.when(b != zz)
        def _():
            sent(b, 5, y_send)
            sent(b, 5, x_send)

        c_copy(b).wait_send()
        out_copy(b).wait()


def scores_of(own, ids, train, devices):
    rows = own.shape[1]
    chunk = own.shape[2]
    examples = train.shape[0]
    line = devices // 2
    dma = pltpu.SemaphoreType.DMA
    return pl.pallas_call(
        functools.partial(score_kernel, line),
        out_shape=jax.ShapeDtypeStruct((line, 2 * rows, examples // 2), jnp.float32),
        in_specs=[
            pl.BlockSpec(memory_space=pltpu.VMEM),
            pl.BlockSpec(memory_space=pltpu.VMEM),
            pl.BlockSpec(memory_space=pl.ANY),
        ],
        out_specs=pl.BlockSpec(memory_space=pl.ANY),
        scratch_shapes=[
            pltpu.VMEM((loads, examples, train.shape[1] // loads), jnp.bfloat16),
            pltpu.VMEM((examples, examples), jnp.bfloat16),
            pltpu.VMEM((chunks, examples, chunk), jnp.bfloat16),
            pltpu.VMEM((line, chunks, 2, rows, chunk), jnp.bfloat16),
            pltpu.VMEM((line, 2, 2 * rows, examples // 2), jnp.float32),
            pltpu.VMEM((line, 2 * rows, examples // 2), jnp.float32),
            pltpu.VMEM((line, 2 * rows, examples // 2), jnp.float32),
            dma((loads,)),
            dma,
            dma((line, 6)),
            dma((line, 5)),
            dma((line, 5)),
            *[dma((line,)) for _ in range(7)],
        ],
        compiler_params=pltpu.CompilerParams(
            collective_id=0, has_side_effects=True, vmem_limit_bytes=56 * 1024 * 1024
        ),
    )(own, ids, train)


def shards(devices, queries, basis_s, basis_a, eigvals, train_grads, example_ids):
    stored = train_grads.reshape(train_grads.shape[0], -1)
    own_rows = precondition(queries, basis_s, basis_a, eigvals)
    rows = own_rows.shape[0]
    cut = own_rows.reshape(rows, chunks, -1).transpose(1, 0, 2)
    scores = scores_of(cut, example_ids, stored, devices)
    return scores.reshape(devices * rows, -1)


def solution(mesh):
    return jax.shard_map(
        functools.partial(shards, mesh.shape["ex"]),
        mesh=mesh,
        in_specs=(
            P("ex", "lay", None),
            P("lay", None, None),
            P("lay", None, None),
            P("lay", None, None),
            P(("grp", "ex"), "lay", None),
            P(("grp", "ex"), None),
        ),
        out_specs=P(None, ("grp", "ex", "lay")),
        check_vma=False,
    )
```

time: 68.6 us -> 62.2 us (0.907)
  Pallas kernels: 53.7 us -> 47.2 us
    pallas_call x1, Pallas kernels: 53.7 us -> 47.2 us  [scores_of(): pl.pallas_call(functools.partial(score_kernel, line), out_shape=jax.Shape...]
    transpose x1 -> x0, local copies, waits for them, and re-layouts: 0.95 us -> none  [shards(): cut = own_rows.reshape(rows, 2 * pairs, -1).transpose(1, 0, 2)]
    convert_element_type x2 -> x3, local copies, waits for them, and re-layouts: 1.27 us -> 2.21 us  [precondition(): restored.reshape(number_rows, layer_count, rank * rank).astype(jnp.bfloat16)]
where the time goes in v1:
time: 62.2 us; the launch traced here: 61.8 us
  Pallas kernels  47.2 us (76%)
  local copies, waits for them, and re-layouts  6.63 us (11%)
  matrix products  5.1 us (8%)
  other arithmetic  2.14 us (3%)
  between operations  0.73 us (1%)
    pallas_call x1, Pallas kernels, scores_of(): pl.pallas_call(functools.partial(score_kernel, line), out_shape=jax.Shape...  47.2 us
    unnamed x5, local copies, waits for them, and re-layouts  2.27 us
    convert_element_type x3, local copies, waits for them, and re-layouts, precondition(): restored.reshape(number_rows, layer_count, rank * rank).astype(jnp.bfloat16)  2.21 us
    dot_general x1, matrix products, precondition(): half_turn = jnp.einsum('nlik,lkm->nlim', expanded, basis_a, precision=high)  2.15 us
    another operation x1, local copies, waits for them, and re-layouts  2.07 us
    reduce_sum x1, other arithmetic, precondition(): damping = damp_ratio * jnp.mean(eigvals, axis=(1, 2), keepdims=True)  1.38 us

profile of v1, /device:TPU:1, one launch (start us, length us, event | category | flops | bytes accessed | tf_op | source)
XLA Modules:
  0.0 61.8 jit_solution(10372505787859090938)
XLA Ops:
  0.0 0.0 copy-start
  0.0 1.4 %reduce_sum.9 = f32[]{:T(128)} reduce(f32[1,64,64]{2,1,0:T(8,128)} %param.9, f32[]{:T(128)} %constant.6.clone.1), dimensions={0,1,2}, to_apply=%region_0.0 | reduce | flops 4095 | bytes 16392 | tf_op jit(solution)/shard_map/reduce_sum | solution.py:25
  2.0 0.8 %add_bitcast_fusion = f32[64,64]{1,0:T(8,128)S(1)} fusion(f32[1,64,64]{2,1,0:T(8,128)} %param.9, f32[]{:T(128)S(6)} %mul.4), kind=kLoop, calls=%fused_computation.14 | loop fusion | flops 4096 | bytes 32772 | tf_op jit(solution)/shard_map/div | solution.py:26
  2.8 0.1 copy.10
  2.9 0.0 copy-start.1
  2.9 2.1 %reshape.49 = bf16[64,64,64]{2,1,0:T(8,128)(2,1)S(1)} reshape(bf16[64,1,4096]{2,0,1:T(8,128)(2,1)} %param.6) | data formatting | bytes 1048576 | tf_op jit(solution)/shard_map/reshape.1
  5.0 0.0 copy-done
  5.0 2.1 %fusion.8 = f32[64,64,64]{2,0,1:T(8,128)S(1)} fusion(bf16[64,64,64]{2,1,0:T(8,128)(2,1)S(1)} %reshape.49, f32[1,64,64]{2,1,0:T(8,128)S(1)} %copy-done), kind=kOutput, calls=%fused_computation.10 | convolution fusion | flops 100663296 | bytes 1589248 | tf_op jit(solution)/shard_map/nlik,lkm->nlim/dot_general | solution.py:23
  7.1 0.0 copy-done.1
  7.1 1.0 %fusion.3 = f32[64,64,64]{2,1,0:T(8,128)S(1)} fusion(f32[64,64,64]{2,0,1:T(8,128)S(1)} %fusion.8, f32[1,64,64]{2,1,0:T(8,128)S(1)} %copy-done.1), kind=kOutput, calls=%fused_computation.3 | convolution fusion | flops 100663296 | bytes 2113536 | tf_op jit(solution)/shard_map/lij,nlim->nljm/dot_general | solution.py:24
  8.1 1.0 %fusion.1 = f32[64,64,64]{1,2,0:T(8,128)S(1)} fusion(f32[64,64,64]{2,1,0:T(8,128)S(1)} %fusion.3, f32[64,64]{0,1:T(8,128)S(1)} %copy.10, f32[1,64,64]{2,1,0:T(8,128)S(1)} %copy-done), kind=kOutput, calls=%fused_computation.2 | convolution fusion | flops 100925440 | bytes 2129920 | tf_op jit(solution)/shard_map/nljm,lpm->nljp/dot_general | solution.py:27
  9.1 1.0 %fusion.5 = bf16[64,1,64,64]{2,3,0,1:T(8,128)(2,1)S(1)} fusion(f32[64,64,64]{1,2,0:T(8,128)S(1)} %fusion.1, f32[1,64,64]{2,1,0:T(8,128)S(1)} %copy-done.1), kind=kOutput, calls=%fused_computation.6 | convolution fusion | flops 100925440 | bytes 1589248 | tf_op jit(solution)/shard_map/lij,nljp->nlip/dot_general | solution.py:28
  10.1 0.7 %copy.11 = bf16[64,1,64,64]{3,2,0,1:T(8,128)(2,1)S(1)} copy(bf16[64,1,64,64]{2,3,0,1:T(8,128)(2,1)S(1)} %fusion.5) | data formatting | bytes 1048576 | tf_op jit(solution)/shard_map/convert_element_type | solution.py:29
  10.8 0.6 convert_element_type.19
  11.4 0.9 %copy.16 = bf16[64,8,512]{2,0,1:T(8,128)(2,1)} copy(bf16[64,8,512]{2,1,0:T(8,128)(2,1)S(1)} %convert_element_type.19) | data formatting | bytes 1048576 | tf_op jit(solution)/shard_map/convert_element_type | solution.py:29
  12.3 47.2 %shard_map.64 = f32[4,128,512]{2,1,0:T(8,128)} custom-call(bf16[8,64,512]{2,1,0:T(8,128)(2,1)} %bitcast.52, s32[1,1024]{1,0:T(1,128)} %ids_ref.1, bf16[1024,4096]{1,0:T(8,128)(2,1)} %bitcast.50), custom_call_target="tpu_custom_call" | custom-call | tf_op jit(solution)/shard_map/pallas_call | solution.py:352
  59.6 2.3 %copy.18 = f32[512,512]{1,0:T(8,128)} copy(f32[512,512]{1,0:T(8,128)} %bitcast.51) | data formatting | bytes 2097152
Async XLA Ops:
  0.0 5.0 %copy-start = (f32[1,64,64]{2,1,0:T(8,128)S(1)}, f32[1,64,64]{2,1,0:T(8,128)}, u32[]{:S(2)}) copy-start(f32[1,64,64]{2,1,0:T(8,128)} %param.8) | copy-start | bytes 49156
  2.9 4.2 %copy-start.1 = (f32[1,64,64]{2,1,0:T(8,128)S(1)}, f32[1,64,64]{2,1,0:T(8,128)}, u32[]{:S(2)}) copy-start(f32[1,64,64]{2,1,0:T(8,128)} %param.7) | copy-start | bytes 49156

commit v2 on v1

--- a/solution.py
+++ b/solution.py
@@ -14,25 +14,113 @@
 MESH = pl.DeviceIdType.MESH
 
 
-def precondition(grads, basis_s, basis_a, eigvals):
-    number_rows = grads.shape[0]
-    layer_count = grads.shape[1]
-    rank = basis_s.shape[-1]
-    high = lax.Precision.HIGH
-    expanded = grads.astype(jnp.float32).reshape(number_rows, layer_count, rank, rank)
-    half_turn = jnp.einsum("nlik,lkm->nlim", expanded, basis_a, precision=high)
-    rotated = jnp.einsum("lij,nlim->nljm", basis_s, half_turn, precision=high)
-    damping = damp_ratio * jnp.mean(eigvals, axis=(1, 2), keepdims=True)
-    scaled = rotated / (eigvals + damping)[None]
-    turned_back = jnp.einsum("nljm,lpm->nljp", scaled, basis_a, precision=high)
-    restored = jnp.einsum("lij,nljp->nlip", basis_s, turned_back, precision=high)
-    return restored.reshape(number_rows, layer_count, rank * rank).astype(jnp.bfloat16)
-
+def split(value):
+    top = value.astype(jnp.bfloat16)
+    return top, (value - top.astype(jnp.float32)).astype(jnp.bfloat16)
+
+
+def ones_where(mask):
+    return jnp.where(mask, 1.0, 0.0).astype(jnp.bfloat16)
+
+
+def picks(shape, rule):
+    return ones_where(rule(lax.broadcasted_iota(jnp.int32, shape, 0), lax.broadcasted_iota(jnp.int32, shape, 1)))
+
+
+def product(a, b, dims=((1,), (0,))):
+    return lax.dot_general(a, b, (dims, ((), ())), preferred_element_type=jnp.float32)
+
+
+across = ((1,), (1,))
+
+
+def twice_diagonal(part, rank):
+    spread = product(part, picks((rank, 2 * rank), lambda r, c: r == c % rank))
+    both = jnp.concatenate([spread, spread], axis=0)
+    shape = (2 * rank, 2 * rank)
+    same = lax.broadcasted_iota(jnp.int32, shape, 0) // rank == lax.broadcasted_iota(jnp.int32, shape, 1) // rank
+    return jnp.where(same, both, 0.0).astype(jnp.bfloat16)
+
+
+def rotate(queries_ref, s_ref, a_ref, eig_ref, turned, stacked):
+    rows = queries_ref.shape[0]
+    rank = s_ref.shape[0]
+    half = rank // 2
+    lane = 2 * rank
+    a_top, a_low = (twice_diagonal(part, rank) for part in split(a_ref[...]))
+    a_both = jnp.concatenate([a_top, a_low], axis=0)
+    for i in range(half):
+        tile = queries_ref[:, i * lane:(i + 1) * lane]
+        turned[i * rows:(i + 1) * rows, :] = product(jnp.concatenate([tile, tile], axis=1), a_both)
+
+    eye = picks((rank, rank), lambda r, c: r == c)
+    s_parts = split(s_ref[...])
+    forward = []
+    back = []
+    for top_or_low, part in enumerate(s_parts):
+        flipped = product(eye, part, across).astype(jnp.bfloat16)
+        sorted_rows = product(picks((rank, rank), lambda r, c: c == (r % half) * 2 + r // half), part).astype(jnp.bfloat16)
+
+        def wanted(c):
+            third = c // half
+            return third < 2 if top_or_low == 0 else third == 2
+
+        forward.append([
+            product(flipped, picks((rank, 3 * half), lambda r, c: (r == 2 * (c % half) + b) & wanted(c)))
+            for b in range(2)
+        ])
+        back.append([
+            product(sorted_rows, picks((rank, 3 * half), lambda r, c: (r == c % half + b * half) & wanted(c)))
+            for b in range(2)
+        ])
+    lhs_forward = jnp.concatenate([forward[0][b] + forward[1][b] for b in range(2)], axis=0).astype(jnp.bfloat16)
+    lhs_back = jnp.concatenate([back[0][b] + back[1][b] for b in range(2)], axis=0).astype(jnp.bfloat16)
+
+    eig = eig_ref[...]
+    damping = damp_ratio * jnp.mean(eig)
+    inverse = 1.0 / (jnp.concatenate([eig[:half], eig[half:]], axis=1) + damping)
+    first = lax.broadcasted_iota(jnp.int32, (half, lane), 1) < rank
+
+    def gather_halves(value):
+        kept = jnp.where(first, value[:half], value[3 * half:])
+        crossed = jnp.where(first, value[half:2 * half], value[2 * half:3 * half])
+        return kept + pltpu.roll(crossed, rank, 1)
+
+    def stack(at, value):
+        top, low = split(value)
+        stacked[0:half, at] = top
+        stacked[half:2 * half, at] = low
+        stacked[2 * half:3 * half, at] = top
+
+    group = 8
+    for base in range(0, rows, group):
+        for n in range(base, base + group):
+            stack(slice(n * lane, (n + 1) * lane), turned[pl.ds(n, half, stride=rows), :])
+    for base in range(0, rows, group):
+        span = slice(base * lane, (base + group) * lane)
+        value = product(lhs_forward, stacked[:, span])
+        for n in range(group):
+            scaled = gather_halves(value[:, n * lane:(n + 1) * lane]) * inverse
+            stack(slice((base + n) * lane, (base + n + 1) * lane), scaled)
+    for base in range(0, rows, group):
+        span = slice(base * lane, (base + group) * lane)
+        value = product(lhs_back, stacked[:, span])
+        for n in range(group):
+            turned[pl.ds(base + n, half, stride=rows), :] = gather_halves(value[:, n * lane:(n + 1) * lane])
+    return jnp.concatenate([a_top, a_top, a_low], axis=1)
+
+
+def condition_chunk(turned, c, rows, per_chunk, a_all, write):
+    lane = turned.shape[1]
+    top, low = split(turned[pl.ds(pl.multiple_of(c * per_chunk * rows, 8), per_chunk * rows), :])
+    value = product(jnp.concatenate([top, low, top], axis=1), a_all, across).astype(jnp.bfloat16)
+    for i in range(per_chunk):
+        write(slice(i * lane, (i + 1) * lane), value[i * rows:(i + 1) * rows])
 
 def score_kernel(
-    line, own_ref, ids_ref, train_ref, out_ref,
-    stored, hot, perm, held, acc, arrived, total,
-    load_sem, own_sem, z_recv, y_recv, x_recv, zr_send, zl_send, y_send, x_send, c_recv, c_send, out_sem,
+    line, queries_ref, s_ref, a_ref, eig_ref, ids_ref, train_ref, out_ref,
+    turned, stacked, stored, hot, perm, held, acc, arrived, total,
+    load_sem, z_recv, y_recv, x_recv, zr_send, zl_send, y_send, x_send, c_recv, c_send, out_sem,
 ):
     grp = lax.axis_index("grp")
     ex = lax.axis_index("ex")
@@ -40,9 +128,9 @@
     zz = ex // 2
     w = ex % 2
     side = grp % 2
-    rows = own_ref.shape[1]
+    rows = queries_ref.shape[0]
     examples = train_ref.shape[0]
-    chunk = own_ref.shape[2]
+    chunk = queries_ref.shape[1] // chunks
     half = examples // 2
     wide = train_ref.shape[1] // loads
     per_load = chunks // loads
@@ -118,13 +206,20 @@
     for target in (across_y, across_x, across_c):
         pl.semaphore_signal(barrier, inc=1, device_id=target, device_id_type=MESH)
 
-    own = pltpu.make_async_copy(own_ref, held.at[zz, :, w], own_sem)
-    own.start()
-    own.wait()
+    a_all = rotate(queries_ref, s_ref, a_ref, eig_ref, turned, stacked)
+
+    def condition(c):
+        def write(at, value):
+            held[zz, c, w, :, at] = value
+
+        condition_chunk(turned, c, rows, chunk // turned.shape[1], a_all, write)
+
     pl.semaphore_wait(barrier, 3 + has_left.astype(jnp.int32) + has_right.astype(jnp.int32))
 
     @pl.loop(0, 6)
     def _(k):
+        condition(z_chunk(k))
+
         @pl.when(has_right)
         def _():
             z_copy(zz, k, zr_send, right).start()
@@ -133,9 +228,17 @@
         def _():
             z_copy(zz, k, zl_send, left).start()
 
-        @pl.when(k < 4)
+        @pl.when(k < 3)
         def _():
             y_copy(zz, k, own_chunk(k), w).start()
+
+        @pl.when(k == 4)
+        def _():
+            y_copy(zz, 3, own_chunk(3), w).start()
+
+    @pl.loop(0, 2)
+    def _(k):
+        condition(2 - 2 * side + k)
 
     spread = jnp.broadcast_to(ids_ref[...].astype(jnp.float32), (128, examples)).T
     lanes = lax.broadcasted_iota(jnp.int32, (examples, 128), 1).astype(jnp.float32)
@@ -343,22 +446,22 @@
         out_copy(b).wait()
 
 
-def scores_of(own, ids, train, devices):
-    rows = own.shape[1]
-    chunk = own.shape[2]
+def scores_of(queries, basis_s, basis_a, eigvals, ids, train, devices):
+    rows = queries.shape[0]
+    chunk = queries.shape[1] // chunks
+    rank = basis_s.shape[0]
     examples = train.shape[0]
     line = devices // 2
     dma = pltpu.SemaphoreType.DMA
+    vmem = pl.BlockSpec(memory_space=pltpu.VMEM)
     return pl.pallas_call(
         functools.partial(score_kernel, line),
         out_shape=jax.ShapeDtypeStruct((line, 2 * rows, examples // 2), jnp.float32),
-        in_specs=[
-            pl.BlockSpec(memory_space=pltpu.VMEM),
-            pl.BlockSpec(memory_space=pltpu.VMEM),
-            pl.BlockSpec(memory_space=pl.ANY),
-        ],
+        in_specs=[vmem] * 5 + [pl.BlockSpec(memory_space=pl.ANY)],
         out_specs=pl.BlockSpec(memory_space=pl.ANY),
         scratch_shapes=[
+            pltpu.VMEM((rank // 2 * rows, 2 * rank), jnp.float32),
+            pltpu.VMEM((3 * rank // 2, rows * 2 * rank), jnp.bfloat16),
             pltpu.VMEM((loads, examples, train.shape[1] // loads), jnp.bfloat16),
             pltpu.VMEM((examples, examples), jnp.bfloat16),
             pltpu.VMEM((chunks, examples, chunk), jnp.bfloat16),
@@ -367,7 +470,6 @@
             pltpu.VMEM((line, 2 * rows, examples // 2), jnp.float32),
             pltpu.VMEM((line, 2 * rows, examples // 2), jnp.float32),
             dma((loads,)),
-            dma,
             dma((line, 6)),
             dma((line, 5)),
             dma((line, 5)),
@@ -376,16 +478,15 @@
         compiler_params=pltpu.CompilerParams(
             collective_id=0, has_side_effects=True, vmem_limit_bytes=56 * 1024 * 1024
         ),
-    )(own, ids, train)
+    )(queries, basis_s, basis_a, eigvals, ids, train)
 
 
 def shards(devices, queries, basis_s, basis_a, eigvals, train_grads, example_ids):
-    stored = train_grads.reshape(train_grads.shape[0], -1)
-    own_rows = precondition(queries, basis_s, basis_a, eigvals)
-    rows = own_rows.shape[0]
-    cut = own_rows.reshape(rows, chunks, -1).transpose(1, 0, 2)
-    scores = scores_of(cut, example_ids, stored, devices)
-    return scores.reshape(devices * rows, -1)
+    scores = scores_of(
+        queries.reshape(queries.shape[0], -1), basis_s[0], basis_a[0], eigvals[0],
+        example_ids, train_grads.reshape(train_grads.shape[0], -1), devices,
+    )
+    return scores.reshape(devices * queries.shape[0], -1)
 
 
 def solution(mesh):

time: 62.2 us -> 51.8 us (0.83)
  matrix products: 5.1 us -> 0 us
  local copies, waits for them, and re-layouts: 6.63 us -> 2.26 us
  Pallas kernels: 47.2 us -> 49.4 us
  other arithmetic: 2.14 us -> 0 us
  between operations: 0.73 us -> 0.01 us
    dot_general x4 -> x0, matrix products: 5.1 us -> none  [the longest x1 2.15 us: precondition(): half_turn = jnp.einsum('nlik,lkm->nlim', expanded, basis_a, precision=high)]
    convert_element_type x3 -> x0, local copies, waits for them, and re-layouts: 2.21 us -> none  [precondition(): restored.reshape(number_rows, layer_count, rank * rank).astype(jnp.bfloat16)]
    pallas_call x1, Pallas kernels: 47.2 us -> 49.4 us  [scores_of(): pl.pallas_call(functools.partial(score_kernel, line), out_shape=jax.Shape...]
    another operation x1 -> x0, local copies, waits for them, and re-layouts: 2.07 us -> none
    reduce_sum x1 -> x0, other arithmetic: 1.38 us -> none  [precondition(): damping = damp_ratio * jnp.mean(eigvals, axis=(1, 2), keepdims=True)]
    div x1 -> x0, other arithmetic: 0.76 us -> none  [precondition(): scaled = rotated / (eigvals + damping)[None]]
    unnamed x5 -> x1, local copies, waits for them, and re-layouts: 2.27 us -> 2.26 us
where the time goes in v2:
time: 51.8 us; the launch traced here: 51.7 us
  Pallas kernels  49.4 us (95%)
  local copies, waits for them, and re-layouts  2.26 us (4%)
    pallas_call x1, Pallas kernels, scores_of(): pl.pallas_call(functools.partial(score_kernel, line), out_shape=jax.Shape...  49.4 us
    unnamed x1, local copies, waits for them, and re-layouts  2.26 us

profile of v2, /device:TPU:1, one launch (start us, length us, event | category | flops | bytes accessed | tf_op | source)
XLA Modules:
  0.0 51.7 jit_solution(5268393480434729721)
XLA Ops:
  0.0 49.4 %shard_map.64 = f32[4,128,512]{2,1,0:T(8,128)} custom-call(bf16[64,4096]{1,0:T(8,128)(2,1)} %bitcast.8, f32[64,64]{1,0:T(8,128)} %bitcast.9, f32[64,64]{1,0:T(8,128)} %bitcast.10, f32[64,64]{1,0:T(8,128)} %bitcast.11, s32[1,1024]{1,0:T(1,128)} %ids_ref.1, bf16[1024,4096]{1,0:T(8,128)(2,1)} %bitcast.6), custom_call_target="tpu_custom_call" | custom-call | tf_op jit(solution)/shard_map/pallas_call | solution.py:457
  49.4 2.3 %copy.8 = f32[512,512]{1,0:T(8,128)} copy(f32[512,512]{1,0:T(8,128)} %bitcast.7) | data formatting | bytes 2097152

commit v3 on v2

--- a/solution.py
+++ b/solution.py
@@ -9,8 +9,7 @@
 
 damp_ratio = 0.1
 chunks = 8
-loads = 4
-window = 256
+slices = 4
 MESH = pl.DeviceIdType.MESH
 
 
@@ -119,7 +118,7 @@
 
 def score_kernel(
     line, queries_ref, s_ref, a_ref, eig_ref, ids_ref, train_ref, out_ref,
-    turned, stacked, stored, hot, perm, held, acc, arrived, total,
+    turned, stacked, stored, hot, held, acc, arrived, total,
     load_sem, z_recv, y_recv, x_recv, zr_send, zl_send, y_send, x_send, c_recv, c_send, out_sem,
 ):
     grp = lax.axis_index("grp")
@@ -132,8 +131,7 @@
     examples = train_ref.shape[0]
     chunk = queries_ref.shape[1] // chunks
     half = examples // 2
-    wide = train_ref.shape[1] // loads
-    per_load = chunks // loads
+    window = examples // slices
     right = {"ex": lax.rem(ex + 2, 2 * line)}
     left = {"ex": lax.rem(ex + 2 * line - 2, 2 * line)}
     across_y = {"ex": zz * 2 + (1 - w)}
@@ -159,9 +157,9 @@
             device_id=target, device_id_type=MESH,
         )
 
-    def load(p):
+    def load(c):
         return pltpu.make_async_copy(
-            train_ref.at[:, pl.ds(p * wide, wide)], stored.at[p], load_sem.at[p]
+            train_ref.at[:, pl.ds(c * chunk, chunk)], stored.at[c], load_sem
         )
 
     def z_copy(b, k, send, target):
@@ -177,7 +175,7 @@
         return remote(slot, slot, x_send.at[b], x_recv.at[b, k], across_x)
 
     def c_copy(b):
-        return remote(acc.at[b, 1 - core], arrived.at[b], c_send.at[b], c_recv.at[b], across_c)
+        return remote(acc.at[b], arrived.at[b], c_send.at[b], c_recv.at[b], across_c)
 
     def out_copy(b):
         return pltpu.make_async_copy(total.at[b], out_ref.at[b], out_sem.at[b])
@@ -189,9 +187,9 @@
         from_left = jnp.where(paired, jnp.asarray(i % 2 == 0).astype(jnp.int32), (lefts > rights).astype(jnp.int32))
         return jnp.where(from_left > 0, zz - t, zz + t)
 
-    @pl.loop(0, loads)
-    def _(p):
-        load(p).start()
+    @pl.loop(0, chunks)
+    def _(c):
+        load(c).start()
 
     barrier = pltpu.get_barrier_semaphore()
 
@@ -240,12 +238,11 @@
     def _(k):
         condition(2 - 2 * side + k)
 
-    spread = jnp.broadcast_to(ids_ref[...].astype(jnp.float32), (128, examples)).T
-    lanes = lax.broadcasted_iota(jnp.int32, (examples, 128), 1).astype(jnp.float32)
+    ids = ids_ref[...].astype(jnp.float32)
+    wanted = jnp.where(core == 0, ids[:, :half], ids[:, half:])
     for tile in range(examples // 128):
-        hot[:, tile * 128:(tile + 1) * 128] = jnp.where(
-            spread == lanes + float(tile * 128), 1.0, 0.0
-        ).astype(jnp.bfloat16)
+        row = lax.broadcasted_iota(jnp.int32, (128, half), 0).astype(jnp.float32) + float(tile * 128)
+        hot[tile * 128:(tile + 1) * 128, :] = jnp.where(row == wanted, 1.0, 0.0).astype(jnp.bfloat16)
 
     def z_arrival(b, k, from_left):
         z_copy(b, k, zr_send, right).wait_recv()
@@ -295,90 +292,81 @@
             def _():
                 x_copy(b, k + 2, z_chunk(k), 1 - w).start()
 
-    def permute(c):
-        p = c // per_load
-        at = c % per_load
-
-        @pl.when(at == 0)
-        def _():
-            load(p).wait()
-
-        columns = pl.ds(pl.multiple_of(at * chunk, chunk), chunk)
-
-        @pl.loop(0, 4)
-        def _(part):
-            quarter = examples // 4
-            picked = pl.ds(part * quarter, quarter)
-            perm[c, picked, :] = jnp.dot(
-                hot[picked, :], stored[p, :, columns], preferred_element_type=jnp.float32
-            ).astype(jnp.bfloat16)
-
-    per_half = half // window
-
-    def terms(b, n, picked):
-        part = pl.ds(pl.multiple_of(n * window, window), window)
+    def window_of(n):
+        return pl.ds(pl.multiple_of(n * window, window), window)
+
+    def terms(blocks, n, picked):
         value = None
         for c in picked:
-            term = lax.dot_general(
-                held[b, c].reshape(2 * rows, chunk), perm[c, part, :],
-                (((1,), (1,)), ((), ())), preferred_element_type=jnp.float32,
-            )
+            queries = [held[b, c].reshape(2 * rows, chunk) for b in blocks]
+            term = product(jnp.concatenate(queries, axis=0), stored[c, window_of(n), :], across)
             value = term if value is None else value + term
-        return value
-
-    def columns_of(n):
-        return n // per_half, pl.ds(pl.multiple_of((n % per_half) * window, window), window)
-
-    def whole_block(b, n):
-        h, at = columns_of(n)
-        acc[b, h, :, at] = terms(b, n, range(chunks))
+        return [value[i * 2 * rows:(i + 1) * 2 * rows] for i in range(len(blocks))]
+
+    def whole(blocks, n):
+        for b, value in zip(blocks, terms(blocks, n, range(chunks))):
+            acc[b, :, window_of(n)] = value
 
     def x_arrivals(b, first, last):
         for k in range(first, last):
             x_copy(b, k, 0, w).wait_recv()
 
+    def all_x_arrivals(b):
+        x_arrivals(b, 0, 4)
+
+        @pl.when(b != zz)
+        def _():
+            x_arrivals(b, 4, 5)
+
     def finish(b):
         c_copy(b).wait_recv()
-        total[b] = acc[b, core] + arrived[b]
+        both = jnp.concatenate(split(acc[b] + arrived[b]), axis=0)
+        value = product(both, hot[...])
+        total[b] = value[:2 * rows] + value[2 * rows:]
         out_copy(b).start()
 
-    tiles = examples // window
-    first_own = 8
+    alone = 6 * (line - 2) + 4
 
     def compute(tick):
-        @pl.when(tick < chunks)
-        def _():
-            permute(tick)
-
-        for at in range(2):
-            @pl.when(tick == first_own + at)
-            def _():
-                if at == 0:
-                    x_arrivals(zz, 0, 4)
-
-                @pl.loop(at * (tiles // 2), (at + 1) * (tiles // 2))
-                def _(n):
-                    whole_block(zz, n)
-
-                if at == 1:
-                    c_copy(zz).start()
-
-            j = (tick - 6 - at) // 6
-
-            @pl.when(jnp.logical_and(tick % 6 == at, jnp.logical_and(tick >= 12, j < line - 1)))
-            def _():
-                b = block_of(j)
-                if at == 0:
-                    x_arrivals(b, 0, 5)
-
-                @pl.loop(at * (tiles // 2), (at + 1) * (tiles // 2))
-                def _(n):
-                    whole_block(b, n)
-
-                if at == 1:
-                    c_copy(b).start()
-
-    ticks = max(6 * (line - 1), 5 * line, 6 * (line - 2) + 8)
+        p = (tick - 12) // 12
+        n = (tick - 12) % 12
+
+        @pl.when(jnp.logical_and(tick >= 12, jnp.logical_and(n < slices, p < line // 2 - 1)))
+        def _():
+            one = jnp.where(p == 0, zz, block_of(2 * p))
+            other = block_of(2 * p + 1)
+
+            @pl.when(n == 0)
+            def _():
+                @pl.when(p == 0)
+                def _():
+                    pltpu.make_async_copy(stored, stored, load_sem).wait()
+
+                all_x_arrivals(one)
+                all_x_arrivals(other)
+
+            whole([one, other], n)
+
+            @pl.when(n == slices - 1)
+            def _():
+                c_copy(one).start()
+                c_copy(other).start()
+
+        @pl.when(jnp.logical_and(tick >= alone, tick < alone + slices))
+        def _():
+            b = block_of(line - 2)
+
+            @pl.when(tick == alone)
+            def _():
+                all_x_arrivals(b)
+
+            whole([b], tick - alone)
+
+            @pl.when(tick == alone + slices - 1)
+            def _():
+                c_copy(b).start()
+
+    ticks = max(6 * (line - 1), 5 * line, alone + slices)
 
     @pl.loop(0, ticks)
     def _(tick):
@@ -390,10 +378,16 @@
     pair = (2 - 2 * side, 3 - 2 * side)
     single = (5 - side,)
 
-    @pl.loop(0, tiles)
+    def add(picked):
+        @pl.loop(0, slices)
+        def _(n):
+            (value,) = terms([last], n, picked)
+            acc[last, :, window_of(n)] = acc[last, :, window_of(n)] + value
+
+    @pl.loop(0, slices)
     def _(n):
-        h, at = columns_of(n)
-        acc[last, h, :, at] = terms(last, n, mine)
+        (value,) = terms([last], n, mine)
+        acc[last, :, window_of(n)] = value
 
     @pl.loop(0, line)
     def _(b):
@@ -402,19 +396,9 @@
             finish(b)
 
     x_arrivals(last, 0, 4)
-
-    @pl.loop(0, tiles)
-    def _(n):
-        h, at = columns_of(n)
-        acc[last, h, :, at] = acc[last, h, :, at] + terms(last, n, pair)
-
+    add(pair)
     x_arrivals(last, 4, 5)
-
-    @pl.loop(0, tiles)
-    def _(n):
-        h, at = columns_of(n)
-        acc[last, h, :, at] = acc[last, h, :, at] + terms(last, n, single)
-
+    add(single)
     c_copy(last).start()
     finish(last)
 
@@ -462,14 +446,13 @@
         scratch_shapes=[
             pltpu.VMEM((rank // 2 * rows, 2 * rank), jnp.float32),
             pltpu.VMEM((3 * rank // 2, rows * 2 * rank), jnp.bfloat16),
-            pltpu.VMEM((loads, examples, train.shape[1] // loads), jnp.bfloat16),
-            pltpu.VMEM((examples, examples), jnp.bfloat16),
             pltpu.VMEM((chunks, examples, chunk), jnp.bfloat16),
+            pltpu.VMEM((examples, examples // 2), jnp.bfloat16),
             pltpu.VMEM((line, chunks, 2, rows, chunk), jnp.bfloat16),
-            pltpu.VMEM((line, 2, 2 * rows, examples // 2), jnp.float32),
+            pltpu.VMEM((line, 2 * rows, examples), jnp.float32),
+            pltpu.VMEM((line, 2 * rows, examples), jnp.float32),
             pltpu.VMEM((line, 2 * rows, examples // 2), jnp.float32),
-            pltpu.VMEM((line, 2 * rows, examples // 2), jnp.float32),
-            dma((loads,)),
+            dma,
             dma((line, 6)),
             dma((line, 5)),
             dma((line, 5)),

time: 51.8 us -> 49.8 us (0.961)
  Pallas kernels: 49.4 us -> 47.4 us
    pallas_call x1, Pallas kernels: 49.4 us -> 47.4 us  [scores_of(): pl.pallas_call(functools.partial(score_kernel, line), out_shape=jax.Shape...]
where the time goes in v3:
time: 49.8 us; the launch traced here: 49.7 us
  Pallas kernels  47.4 us (95%)
  local copies, waits for them, and re-layouts  2.26 us (5%)
    pallas_call x1, Pallas kernels, scores_of(): pl.pallas_call(functools.partial(score_kernel, line), out_shape=jax.Shape...  47.4 us
    unnamed x1, local copies, waits for them, and re-layouts  2.26 us

profile of v3, /device:TPU:1, one launch (start us, length us, event | category | flops | bytes accessed | tf_op | source)
XLA Modules:
  0.0 49.7 jit_solution(8285047071357853053)
XLA Ops:
  0.0 47.4 %shard_map.64 = f32[4,128,512]{2,1,0:T(8,128)} custom-call(bf16[64,4096]{1,0:T(8,128)(2,1)} %bitcast.8, f32[64,64]{1,0:T(8,128)} %bitcast.9, f32[64,64]{1,0:T(8,128)} %bitcast.10, f32[64,64]{1,0:T(8,128)} %bitcast.11, s32[1,1024]{1,0:T(1,128)} %ids_ref.1, bf16[1024,4096]{1,0:T(8,128)(2,1)} %bitcast.6), custom_call_target="tpu_custom_call" | custom-call | tf_op jit(solution)/shard_map/pallas_call | solution.py:441
  47.4 2.3 %copy.8 = f32[512,512]{1,0:T(8,128)} copy(f32[512,512]{1,0:T(8,128)} %bitcast.7) | data formatting | bytes 2097152

commit v4 on v3

--- a/solution.py
+++ b/solution.py
@@ -117,9 +117,9 @@
         write(slice(i * lane, (i + 1) * lane), value[i * rows:(i + 1) * rows])
 
 def score_kernel(
-    line, queries_ref, s_ref, a_ref, eig_ref, ids_ref, train_ref, out_ref,
-    turned, stacked, stored, hot, held, acc, arrived, total,
-    load_sem, z_recv, y_recv, x_recv, zr_send, zl_send, y_send, x_send, c_recv, c_send, out_sem,
+    line, queries_ref, s_ref, a_ref, eig_ref, ids_ref, train_ref, total, acc, arrived, hot,
+    turned, stacked, stored, held,
+    load_sem, z_recv, y_recv, x_recv, zr_send, zl_send, y_send, x_send, c_recv, c_send,
 ):
     grp = lax.axis_index("grp")
     ex = lax.axis_index("ex")
@@ -177,9 +177,6 @@
     def c_copy(b):
         return remote(acc.at[b], arrived.at[b], c_send.at[b], c_recv.at[b], across_c)
 
-    def out_copy(b):
-        return pltpu.make_async_copy(total.at[b], out_ref.at[b], out_sem.at[b])
-
     def block_of(j):
         i = j - 1
         paired = i < 2 * both_ways
@@ -323,7 +320,6 @@
         both = jnp.concatenate(split(acc[b] + arrived[b]), axis=0)
         value = product(both, hot[...])
         total[b] = value[:2 * rows] + value[2 * rows:]
-        out_copy(b).start()
 
     alone = 6 * (line - 2) + 4
 
@@ -400,7 +396,7 @@
     x_arrivals(last, 4, 5)
     add(single)
     c_copy(last).start()
-    finish(last)
+    c_copy(last).wait_recv()
 
     def sent(b, count, send):
         span = held.at[b, pl.ds(0, count), w]
@@ -427,7 +423,6 @@
             sent(b, 5, x_send)
 
         c_copy(b).wait_send()
-        out_copy(b).wait()
 
 
 def scores_of(queries, basis_s, basis_a, eigvals, ids, train, devices):
@@ -440,36 +435,82 @@
     vmem = pl.BlockSpec(memory_space=pltpu.VMEM)
     return pl.pallas_call(
         functools.partial(score_kernel, line),
-        out_shape=jax.ShapeDtypeStruct((line, 2 * rows, examples // 2), jnp.float32),
-        in_specs=[vmem] * 5 + [pl.BlockSpec(memory_space=pl.ANY)],
-        out_specs=pl.BlockSpec(memory_space=pl.ANY),
+        out_shape=[
+            pltpu.VMEM((line, 2 * rows, examples // 2), jnp.float32),
+            pltpu.VMEM((line, 2 * rows, examples), jnp.float32),
+            pltpu.VMEM((line, 2 * rows, examples), jnp.float32),
+            pltpu.VMEM((examples, examples // 2), jnp.bfloat16),
+        ],
+        in_specs=[vmem] * 5 + [pl.BlockSpec(memory_space=pltpu.HBM)],
+        out_specs=[vmem] * 4,
         scratch_shapes=[
             pltpu.VMEM((rank // 2 * rows, 2 * rank), jnp.float32),
             pltpu.VMEM((3 * rank // 2, rows * 2 * rank), jnp.bfloat16),
             pltpu.VMEM((chunks, examples, chunk), jnp.bfloat16),
-            pltpu.VMEM((examples, examples // 2), jnp.bfloat16),
             pltpu.VMEM((line, chunks, 2, rows, chunk), jnp.bfloat16),
-            pltpu.VMEM((line, 2 * rows, examples), jnp.float32),
-            pltpu.VMEM((line, 2 * rows, examples), jnp.float32),
-            pltpu.VMEM((line, 2 * rows, examples // 2), jnp.float32),
             dma,
             dma((line, 6)),
             dma((line, 5)),
             dma((line, 5)),
-            *[dma((line,)) for _ in range(7)],
+            *[dma((line,)) for _ in range(6)],
         ],
         compiler_params=pltpu.CompilerParams(
-            collective_id=0, has_side_effects=True, vmem_limit_bytes=56 * 1024 * 1024
+            collective_id=0, has_side_effects=True, vmem_limit_bytes=52 * 1024 * 1024
         ),
     )(queries, basis_s, basis_a, eigvals, ids, train)
 
 
+def last_of(line):
+    zz = lax.axis_index("ex") // 2
+    return jnp.where(zz > line - 1 - zz, 0, line - 1)
+
+
+def finish_kernel(line, total_ref, acc_ref, arrived_ref, hot_ref, out_ref, done, sems):
+    zz = lax.axis_index("ex") // 2
+    last = jnp.where(zz > line - 1 - zz, 0, line - 1)
+    rows = total_ref.shape[1]
+
+    def out_copy(b, source):
+        return pltpu.make_async_copy(source, out_ref.at[b], sems.at[b])
+
+    @pl.loop(0, line)
+    def _(b):
+        @pl.when(b != last)
+        def _():
+            out_copy(b, total_ref.at[b]).start()
+
+    both = jnp.concatenate(split(acc_ref[last] + arrived_ref[last]), axis=0)
+    value = product(both, hot_ref[...])
+    done[...] = value[:rows] + value[rows:]
+    out_copy(last, done).start()
+
+    @pl.loop(0, line)
+    def _(b):
+        out_copy(b, done).wait()
+
+
+def finished(total, acc, arrived, hot):
+    line = total.shape[0]
+    vmem = pl.BlockSpec(memory_space=pltpu.VMEM)
+    return pl.pallas_call(
+        functools.partial(finish_kernel, line),
+        out_shape=jax.ShapeDtypeStruct(total.shape, jnp.float32),
+        in_specs=[vmem] * 4,
+        out_specs=pl.BlockSpec(memory_space=pl.ANY),
+        scratch_shapes=[
+            pltpu.VMEM(total.shape[1:], jnp.float32),
+            pltpu.SemaphoreType.DMA((line,)),
+        ],
+        compiler_params=pltpu.CompilerParams(vmem_limit_bytes=8 * 1024 * 1024),
+    )(total, acc, arrived, hot)
+
+
 def shards(devices, queries, basis_s, basis_a, eigvals, train_grads, example_ids):
-    scores = scores_of(
+    parts = scores_of(
         queries.reshape(queries.shape[0], -1), basis_s[0], basis_a[0], eigvals[0],
         example_ids, train_grads.reshape(train_grads.shape[0], -1), devices,
     )
-    return scores.reshape(devices * queries.shape[0], -1)
+    return finished(*parts).reshape(devices * queries.shape[0], -1)
 
 
 def solution(mesh):

time: 49.8 us -> 47.7 us (0.958)
  local copies, waits for them, and re-layouts: 2.26 us -> 0 us
    unnamed x1 -> x0, local copies, waits for them, and re-layouts: 2.26 us -> none
    pallas_call x1 -> x2, Pallas kernels: 47.4 us -> 47.5 us  [the longest x1 46.2 us: scores_of(): pl.pallas_call(functools.partial(score_kernel, line), out_shape=[pltpu.VM...]
where the time goes in v4:
time: 47.7 us; the launch traced here: 47.5 us
  Pallas kernels  47.5 us (100%)
    pallas_call x1, Pallas kernels, scores_of(): pl.pallas_call(functools.partial(score_kernel, line), out_shape=[pltpu.VM...  46.2 us
    pallas_call x1, Pallas kernels, finished(): pl.pallas_call(functools.partial(finish_kernel, line), out_shape=jax.Shap...  1.22 us

profile of v4, /device:TPU:1, one launch (start us, length us, event | category | flops | bytes accessed | tf_op | source)
XLA Modules:
  0.0 47.5 jit_solution(5190647785038649819)
XLA Ops:
  0.0 46.2 %shard_map.64 = (f32[4,128,512]{2,1,0:T(8,128)S(1)}, f32[4,128,1024]{2,1,0:T(8,128)S(1)}, f32[4,128,1024]{2,1,0:T(8,128)S(1)}, bf16[1024,512]{1,0:T(8,128)(2,1)S(1)}) custom-call(bf16[64,4096]{1,0:T(8,128)(2,1)} %bitcast.7, f32[64,64]{1,0:T(8,128)} %bitcast.8, f32[64,64]{1,0:T(8,128)} %bitcast.9, f32[64,64]{1,0:T(8,128)} %bitcast.10, s32[1,1024]{1,0:T(1,128)} %ids_ref.1, ...), custom_call_target="tpu_custom_call" | custom-call | tf_op jit(solution)/shard_map/pallas_call | solution.py:436
  46.3 1.2 %shard_map.65 = f32[4,128,512]{2,1,0:T(8,128)} custom-call(f32[4,128,512]{2,1,0:T(8,128)S(1)} %get-tuple-element.9.total_ref, f32[4,128,1024]{2,1,0:T(8,128)S(1)} %get-tuple-element.10.acc_ref, f32[4,128,1024]{2,1,0:T(8,128)S(1)} %get-tuple-element.11.arrived_ref, bf16[1024,512]{1,0:T(8,128)(2,1)S(1)} %get-tuple-element.12.hot_ref), custom_call_target="tpu_custom_call" | custom-call | tf_op jit(solution)/shard_map/pallas_call | solution.py:495

commit v5 on v4

--- a/solution.py
+++ b/solution.py
@@ -10,6 +10,8 @@
 damp_ratio = 0.1
 chunks = 8
 slices = 4
+late = 12
+own_tick = 9
 MESH = pl.DeviceIdType.MESH
 
 
@@ -115,6 +117,17 @@
     value = product(jnp.concatenate([top, low, top], axis=1), a_all, across).astype(jnp.bfloat16)
     for i in range(per_chunk):
         write(slice(i * lane, (i + 1) * lane), value[i * rows:(i + 1) * rows])
+
+def nth_block(j, zz, line):
+    lefts = zz
+    rights = line - 1 - zz
+    both_ways = jnp.minimum(lefts, rights)
+    i = j - 1
+    paired = i < 2 * both_ways
+    t = jnp.where(paired, i // 2 + 1, j - both_ways)
+    from_left = jnp.where(paired, jnp.asarray(i % 2 == 0).astype(jnp.int32), (lefts > rights).astype(jnp.int32))
+    return jnp.where(from_left > 0, zz - t, zz + t)
+
 
 def score_kernel(
     line, queries_ref, s_ref, a_ref, eig_ref, ids_ref, train_ref, total, acc, arrived, hot,
@@ -139,13 +152,13 @@
     across_c = {"lay": 1 - core}
     has_left = zz > 0
     has_right = zz < line - 1
-    lefts = zz
-    rights = line - 1 - zz
-    both_ways = jnp.minimum(lefts, rights)
+    both_ways = jnp.minimum(zz, line - 1 - zz)
 
     def z_chunk(k):
         return jnp.where(
-            k < 2, 2 * side + k, jnp.where(k == 2, 4 + side, jnp.where(k < 5, 3 + k, 5 - side))
+            k < 2, 2 * side + k, jnp.where(
+                k == 2, 4 + side, jnp.where(k < 5, 3 + k, jnp.where(k == 5, 5 - side, 3 - 2 * side))
+            )
         )
 
     def own_chunk(k):
@@ -178,11 +191,7 @@
         return remote(acc.at[b], arrived.at[b], c_send.at[b], c_recv.at[b], across_c)
 
     def block_of(j):
-        i = j - 1
-        paired = i < 2 * both_ways
-        t = jnp.where(paired, i // 2 + 1, j - both_ways)
-        from_left = jnp.where(paired, jnp.asarray(i % 2 == 0).astype(jnp.int32), (lefts > rights).astype(jnp.int32))
-        return jnp.where(from_left > 0, zz - t, zz + t)
+        return nth_block(j, zz, line)
 
     @pl.loop(0, chunks)
     def _(c):
@@ -211,17 +220,19 @@
 
     pl.semaphore_wait(barrier, 3 + has_left.astype(jnp.int32) + has_right.astype(jnp.int32))
 
+    def send_z(k):
+        @pl.when(has_right)
+        def _():
+            z_copy(zz, k, zr_send, right).start()
+
+        @pl.when(has_left)
+        def _():
+            z_copy(zz, k, zl_send, left).start()
+
     @pl.loop(0, 6)
     def _(k):
         condition(z_chunk(k))
-
-        @pl.when(has_right)
-        def _():
-            z_copy(zz, k, zr_send, right).start()
-
-        @pl.when(has_left)
-        def _():
-            z_copy(zz, k, zl_send, left).start()
+        send_z(k)
 
         @pl.when(k < 3)
         def _():
@@ -241,7 +252,7 @@
         row = lax.broadcasted_iota(jnp.int32, (128, half), 0).astype(jnp.float32) + float(tile * 128)
         hot[tile * 128:(tile + 1) * 128, :] = jnp.where(row == wanted, 1.0, 0.0).astype(jnp.bfloat16)
 
-    def z_arrival(b, k, from_left):
+    def z_arrival(b, k, from_left, near):
         z_copy(b, k, zr_send, right).wait_recv()
         if from_left:
             @pl.when(has_right)
@@ -256,9 +267,21 @@
         def _():
             y_copy(b, k, z_chunk(k), w).start()
 
-        @pl.when(k < 2)
+        @pl.when(jnp.logical_or(k == 0, jnp.logical_and(k == 1, jnp.logical_not(near))))
         def _():
             x_copy(b, k, z_chunk(k), w).start()
+
+    def y_arrival(r):
+        shared = r < 10 * both_ways
+        t = r // 10 + 1
+        near = jnp.where(r % 2 == 0, zz - t, zz + t)
+        b = jnp.where(shared, near, block_of(r // 5 + 1))
+        k = jnp.where(shared, r % 10 // 2, r % 5)
+        y_copy(b, k, z_chunk(k), 1 - w).wait_recv()
+
+        @pl.when(k < 3)
+        def _():
+            x_copy(b, k + 2, z_chunk(k), 1 - w).start()
 
     def relay(tick):
         t = tick // 6 + 1
@@ -266,28 +289,26 @@
 
         @pl.when(jnp.logical_and(t < line, zz - t >= 0))
         def _():
-            z_arrival(zz - t, k, True)
+            z_arrival(zz - t, k, True, t == 1)
 
         @pl.when(jnp.logical_and(t < line, zz + t < line))
         def _():
-            z_arrival(zz + t, k, False)
-
-        q = tick - 1
-
-        @pl.when(jnp.logical_and(q >= 0, q < 4))
+            z_arrival(zz + t, k, False, t == 1)
+
+        @pl.when(jnp.asarray(tick) == late)
+        def _():
+            send_z(6)
+
+        q = tick
+
+        @pl.when(q < 4)
         def _():
             y_copy(zz, q, own_chunk(q), 1 - w).wait_recv()
             x_copy(zz, q, own_chunk(q), 1 - w).start()
 
-        @pl.when(jnp.logical_and(q >= 4, q < 4 + 5 * (line - 1)))
-        def _():
-            b = block_of((q - 4) // 5 + 1)
-            k = (q - 4) % 5
-            y_copy(b, k, z_chunk(k), 1 - w).wait_recv()
-
-            @pl.when(k < 3)
-            def _():
-                x_copy(b, k + 2, z_chunk(k), 1 - w).start()
+        @pl.when(jnp.logical_and(q >= 4, q < 5 * line - 2))
+        def _():
+            y_arrival(q - 4)
 
     def window_of(n):
         return pl.ds(pl.multiple_of(n * window, window), window)
@@ -300,20 +321,27 @@
             value = term if value is None else value + term
         return [value[i * 2 * rows:(i + 1) * 2 * rows] for i in range(len(blocks))]
 
-    def whole(blocks, n):
-        for b, value in zip(blocks, terms(blocks, n, range(chunks))):
-            acc[b, :, window_of(n)] = value
-
-    def x_arrivals(b, first, last):
-        for k in range(first, last):
+    def put(blocks, n, picked, more=False):
+        for b, value in zip(blocks, terms(blocks, n, picked)):
+            acc[b, :, window_of(n)] = acc[b, :, window_of(n)] + value if more else value
+
+    def last_arrivals(b):
+        x_copy(b, 0, 0, w).wait_recv()
+        for k in (2, 3):
             x_copy(b, k, 0, w).wait_recv()
-
-    def all_x_arrivals(b):
-        x_arrivals(b, 0, 4)
+        near = jnp.abs(b - zz) == 1
+
+        @pl.when(near)
+        def _():
+            z_copy(b, 6, zr_send, right).wait_recv()
+
+        @pl.when(jnp.logical_not(near))
+        def _():
+            x_copy(b, 1, 0, w).wait_recv()
 
         @pl.when(b != zz)
         def _():
-            x_arrivals(b, 4, 5)
+            x_copy(b, 4, 0, w).wait_recv()
 
     def finish(b):
         c_copy(b).wait_recv()
@@ -321,80 +349,89 @@
         value = product(both, hot[...])
         total[b] = value[:2 * rows] + value[2 * rows:]
 
-    alone = 6 * (line - 2) + 4
+    mine = (2 * side, 2 * side + 1, 4 + side, 6, 7)
+    pair = (2 - 2 * side, 3 - 2 * side)
+    single = (5 - side,)
+    last = block_of(line - 1)
+    ticks = max(6 * (line - 1), 5 * line - 2)
 
     def compute(tick):
-        p = (tick - 12) // 12
-        n = (tick - 12) % 12
-
-        @pl.when(jnp.logical_and(tick >= 12, jnp.logical_and(n < slices, p < line // 2 - 1)))
-        def _():
-            one = jnp.where(p == 0, zz, block_of(2 * p))
-            other = block_of(2 * p + 1)
-
+        n = tick - own_tick
+
+        @pl.when(jnp.logical_and(n >= 0, n < slices))
+        def _():
             @pl.when(n == 0)
             def _():
-                @pl.when(p == 0)
-                def _():
-                    pltpu.make_async_copy(stored, stored, load_sem).wait()
-
-                all_x_arrivals(one)
-                all_x_arrivals(other)
-
-            whole([one, other], n)
+                pltpu.make_async_copy(stored, stored, load_sem).wait()
+                for k in range(4):
+                    x_copy(zz, k, 0, w).wait_recv()
+
+            put([zz], n, range(chunks))
 
             @pl.when(n == slices - 1)
             def _():
-                c_copy(one).start()
-                c_copy(other).start()
-
-        @pl.when(jnp.logical_and(tick >= alone, tick < alone + slices))
-        def _():
-            b = block_of(line - 2)
-
-            @pl.when(tick == alone)
-            def _():
-                all_x_arrivals(b)
-
-            whole([b], tick - alone)
-
-            @pl.when(tick == alone + slices - 1)
-            def _():
-                c_copy(b).start()
-
-    ticks = max(6 * (line - 1), 5 * line, alone + slices)
+                c_copy(zz).start()
+
+        @pl.when(tick == own_tick + 6)
+        def _():
+            finish(zz)
+
+        p = (tick - 1) // 12
+        step = (tick - 1) % 12
+        one = block_of(2 * p - 1)
+        other = block_of(2 * p)
+        inside = jnp.logical_and(p >= 1, p < line // 2)
+
+        @pl.when(jnp.logical_and(inside, step < 2))
+        def _():
+            @pl.loop(2 * step, 2 * step + 2)
+            def _(m):
+                put([one, other], m, mine)
+
+        @pl.when(jnp.logical_and(inside, step == 3))
+        def _():
+            last_arrivals(one)
+            last_arrivals(other)
+
+            @pl.loop(0, slices)
+            def _(m):
+                put([one, other], m, pair + single, True)
+
+            c_copy(one).start()
+            c_copy(other).start()
+
+        @pl.when(jnp.logical_and(inside, jnp.logical_and(step == 9, p < line // 2 - 1)))
+        def _():
+            finish(one)
+            finish(other)
 
     @pl.loop(0, ticks)
     def _(tick):
         relay(tick)
         compute(tick)
 
-    last = block_of(line - 1)
-    mine = (2 * side, 2 * side + 1, 4 + side, 6, 7)
-    pair = (2 - 2 * side, 3 - 2 * side)
-    single = (5 - side,)
-
-    def add(picked):
-        @pl.loop(0, slices)
-        def _(n):
-            (value,) = terms([last], n, picked)
-            acc[last, :, window_of(n)] = acc[last, :, window_of(n)] + value
-
     @pl.loop(0, slices)
-    def _(n):
-        (value,) = terms([last], n, mine)
-        acc[last, :, window_of(n)] = value
-
-    @pl.loop(0, line)
-    def _(b):
-        @pl.when(b != last)
-        def _():
-            finish(b)
-
-    x_arrivals(last, 0, 4)
-    add(pair)
-    x_arrivals(last, 4, 5)
-    add(single)
+    def _(m):
+        put([last], m, mine[:4])
+
+    y_arrival(5 * line - 6)
+
+    for k in range(4):
+        x_copy(last, k, 0, w).wait_recv()
+
+    @pl.loop(0, slices)
+    def _(m):
+        put([last], m, mine[4:] + pair, True)
+
+    x_copy(last, 4, 0, w).wait_recv()
+
+    @pl.loop(0, slices)
+    def _(m):
+        put([last], m, single, True)
+
+    for j in (line - 3, line - 2):
+        c_copy(block_of(j)).wait_recv()
+
     c_copy(last).start()
     c_copy(last).wait_recv()
 
@@ -404,23 +441,38 @@
 
     @pl.loop(0, line)
     def _(b):
-        @pl.when(jnp.logical_and(has_right, b <= zz))
+        @pl.when(jnp.logical_and(has_right, b < zz))
         def _():
             sent(b, 6, zr_send)
 
-        @pl.when(jnp.logical_and(has_left, b >= zz))
+        @pl.when(jnp.logical_and(has_left, b > zz))
         def _():
             sent(b, 6, zl_send)
 
         @pl.when(b == zz)
         def _():
+            @pl.when(has_right)
+            def _():
+                sent(b, 7, zr_send)
+
+            @pl.when(has_left)
+            def _():
+                sent(b, 7, zl_send)
+
             sent(b, 4, y_send)
             sent(b, 4, x_send)
 
         @pl.when(b != zz)
         def _():
             sent(b, 5, y_send)
-            sent(b, 5, x_send)
+
+            @pl.when(jnp.abs(b - zz) == 1)
+            def _():
+                sent(b, 4, x_send)
+
+            @pl.when(jnp.abs(b - zz) != 1)
+            def _():
+                sent(b, 5, x_send)
 
         c_copy(b).wait_send()
 
@@ -449,7 +501,7 @@
             pltpu.VMEM((chunks, examples, chunk), jnp.bfloat16),
             pltpu.VMEM((line, chunks, 2, rows, chunk), jnp.bfloat16),
             dma,
-            dma((line, 6)),
+            dma((line, 7)),
             dma((line, 5)),
             dma((line, 5)),
             *[dma((line,)) for _ in range(6)],
@@ -460,33 +512,34 @@
     )(queries, basis_s, basis_a, eigvals, ids, train)
 
 
-def last_of(line):
-    zz = lax.axis_index("ex") // 2
-    return jnp.where(zz > line - 1 - zz, 0, line - 1)
-
-
 def finish_kernel(line, total_ref, acc_ref, arrived_ref, hot_ref, out_ref, done, sems):
     zz = lax.axis_index("ex") // 2
-    last = jnp.where(zz > line - 1 - zz, 0, line - 1)
     rows = total_ref.shape[1]
+    open_blocks = [nth_block(j, zz, line) for j in (line - 3, line - 2, line - 1)]
 
     def out_copy(b, source):
         return pltpu.make_async_copy(source, out_ref.at[b], sems.at[b])
 
     @pl.loop(0, line)
     def _(b):
-        @pl.when(b != last)
+        ready = jnp.logical_and(b != open_blocks[0], jnp.logical_and(b != open_blocks[1], b != open_blocks[2]))
+
+        @pl.when(ready)
         def _():
             out_copy(b, total_ref.at[b]).start()
 
-    both = jnp.concatenate(split(acc_ref[last] + arrived_ref[last]), axis=0)
-    value = product(both, hot_ref[...])
-    done[...] = value[:rows] + value[rows:]
-    out_copy(last, done).start()
+    for base, group in ((0, open_blocks[:2]), (2, open_blocks[2:])):
+        both = jnp.concatenate([acc_ref[b] + arrived_ref[b] for b in group], axis=0)
+        value = product(jnp.concatenate(split(both), axis=0), hot_ref[...])
+        half = both.shape[0]
+        value = value[:half] + value[half:]
+        for i, b in enumerate(group):
+            done[base + i] = value[i * rows:(i + 1) * rows]
+            out_copy(b, done.at[base + i]).start()
 
     @pl.loop(0, line)
     def _(b):
-        out_copy(b, done).wait()
+        out_copy(b, done.at[0]).wait()
 
 
 def finished(total, acc, arrived, hot):
@@ -498,7 +551,7 @@
         in_specs=[vmem] * 4,
         out_specs=pl.BlockSpec(memory_space=pl.ANY),
         scratch_shapes=[
-            pltpu.VMEM(total.shape[1:], jnp.float32),
+            pltpu.VMEM((3, *total.shape[1:]), jnp.float32),
             pltpu.SemaphoreType.DMA((line,)),
         ],
         compiler_params=pltpu.CompilerParams(vmem_limit_bytes=8 * 1024 * 1024),

time: 47.7 us -> 45.5 us (0.954)
  Pallas kernels: 47.5 us -> 45.3 us
    pallas_call x1, Pallas kernels: 46.2 us -> 43.5 us  [scores_of(): pl.pallas_call(functools.partial(score_kernel, line), out_shape=[pltpu.VM...]
    pallas_call x1, Pallas kernels: 1.22 us -> 1.77 us  [finished(): pl.pallas_call(functools.partial(finish_kernel, line), out_shape=jax.Shap...]
where the time goes in v5:
time: 45.5 us; the launch traced here: 45.3 us
  Pallas kernels  45.3 us (100%)
    pallas_call x1, Pallas kernels, scores_of(): pl.pallas_call(functools.partial(score_kernel, line), out_shape=[pltpu.VM...  43.5 us
    pallas_call x1, Pallas kernels, finished(): pl.pallas_call(functools.partial(finish_kernel, line), out_shape=jax.Shap...  1.77 us

profile of v5, /device:TPU:1, one launch (start us, length us, event | category | flops | bytes accessed | tf_op | source)
XLA Modules:
  0.0 45.3 jit_solution(5968884836065228598)
XLA Ops:
  0.0 43.5 %shard_map.64 = (f32[4,128,512]{2,1,0:T(8,128)S(1)}, f32[4,128,1024]{2,1,0:T(8,128)S(1)}, f32[4,128,1024]{2,1,0:T(8,128)S(1)}, bf16[1024,512]{1,0:T(8,128)(2,1)S(1)}) custom-call(bf16[64,4096]{1,0:T(8,128)(2,1)} %bitcast.7, f32[64,64]{1,0:T(8,128)} %bitcast.8, f32[64,64]{1,0:T(8,128)} %bitcast.9, f32[64,64]{1,0:T(8,128)} %bitcast.10, s32[1,1024]{1,0:T(1,128)} %ids_ref.1, ...), custom_call_target="tpu_custom_call" | custom-call | tf_op jit(solution)/shard_map/pallas_call | solution.py:488
  43.5 1.8 %shard_map.65 = f32[4,128,512]{2,1,0:T(8,128)} custom-call(f32[4,128,512]{2,1,0:T(8,128)S(1)} %get-tuple-element.9.total_ref, f32[4,128,1024]{2,1,0:T(8,128)S(1)} %get-tuple-element.10.acc_ref, f32[4,128,1024]{2,1,0:T(8,128)S(1)} %get-tuple-element.11.arrived_ref, bf16[1024,512]{1,0:T(8,128)(2,1)S(1)} %get-tuple-element.12.hot_ref), custom_call_target="tpu_custom_call" | custom-call | tf_op jit(solution)/shard_map/pallas_call | solution.py:548

commit v6 on v5

--- a/solution.py
+++ b/solution.py
@@ -9,7 +9,8 @@
 
 damp_ratio = 0.1
 chunks = 8
-slices = 4
+slices = 2
+edge = 256
 late = 12
 own_tick = 9
 MESH = pl.DeviceIdType.MESH
@@ -131,7 +132,7 @@
 
 def score_kernel(
     line, queries_ref, s_ref, a_ref, eig_ref, ids_ref, train_ref, total, acc, arrived, hot,
-    turned, stacked, stored, held,
+    turned, stacked, stored, turned_train, held,
     load_sem, z_recv, y_recv, x_recv, zr_send, zl_send, y_send, x_send, c_recv, c_send,
 ):
     grp = lax.axis_index("grp")
@@ -310,20 +311,29 @@
         def _():
             y_arrival(q - 4)
 
-    def window_of(n):
-        return pl.ds(pl.multiple_of(n * window, window), window)
-
-    def terms(blocks, n, picked):
+    def turn_train(c):
+        eye = picks((edge, edge), lambda r, c: r == c)
+        for at in range(0, chunk, edge):
+            for n in range(slices):
+                columns = slice(n * window, (n + 1) * window)
+                turned_train[c, at:at + edge, columns] = product(
+                    eye, stored[c, columns, at:at + edge], across
+                ).astype(jnp.bfloat16)
+
+    def put(blocks, n, picked, more=False):
+        columns = slice(n * window, (n + 1) * window)
         value = None
         for c in picked:
             queries = [held[b, c].reshape(2 * rows, chunk) for b in blocks]
-            term = product(jnp.concatenate(queries, axis=0), stored[c, window_of(n), :], across)
+            term = product(jnp.concatenate(queries, axis=0), turned_train[c, :, columns])
             value = term if value is None else value + term
-        return [value[i * 2 * rows:(i + 1) * 2 * rows] for i in range(len(blocks))]
-
-    def put(blocks, n, picked, more=False):
-        for b, value in zip(blocks, terms(blocks, n, picked)):
-            acc[b, :, window_of(n)] = acc[b, :, window_of(n)] + value if more else value
+        for i, b in enumerate(blocks):
+            part = value[i * 2 * rows:(i + 1) * 2 * rows]
+            acc[b, :, columns] = acc[b, :, columns] + part if more else part
+
+    def put_all(blocks, picked, more=False):
+        for n in range(slices):
+            put(blocks, n, picked, more)
 
     def last_arrivals(b):
         x_copy(b, 0, 0, w).wait_recv()
@@ -356,21 +366,25 @@
     ticks = max(6 * (line - 1), 5 * line - 2)
 
     def compute(tick):
-        n = tick - own_tick
-
-        @pl.when(jnp.logical_and(n >= 0, n < slices))
-        def _():
-            @pl.when(n == 0)
+        @pl.when(tick < chunks)
+        def _():
+            @pl.when(tick == 0)
             def _():
                 pltpu.make_async_copy(stored, stored, load_sem).wait()
-                for k in range(4):
-                    x_copy(zz, k, 0, w).wait_recv()
-
-            put([zz], n, range(chunks))
-
-            @pl.when(n == slices - 1)
-            def _():
-                c_copy(zz).start()
+
+            turn_train(tick)
+
+        for n in range(slices):
+            @pl.when(tick == own_tick + n)
+            def _():
+                if n == 0:
+                    for k in range(4):
+                        x_copy(zz, k, 0, w).wait_recv()
+
+                put([zz], n, range(chunks))
+
+                if n == slices - 1:
+                    c_copy(zz).start()
 
         @pl.when(tick == own_tick + 6)
         def _():
@@ -382,20 +396,17 @@
         other = block_of(2 * p)
         inside = jnp.logical_and(p >= 1, p < line // 2)
 
-        @pl.when(jnp.logical_and(inside, step < 2))
-        def _():
-            @pl.loop(2 * step, 2 * step + 2)
-            def _(m):
-                put([one, other], m, mine)
+        for n in range(slices):
+            @pl.when(jnp.logical_and(inside, step == n))
+            def _():
+                put([one, other], n, mine)
 
         @pl.when(jnp.logical_and(inside, step == 3))
         def _():
             last_arrivals(one)
             last_arrivals(other)
 
-            @pl.loop(0, slices)
-            def _(m):
-                put([one, other], m, pair + single, True)
+            put_all([one, other], pair + single, True)
 
             c_copy(one).start()
             c_copy(other).start()
@@ -410,24 +421,18 @@
         relay(tick)
         compute(tick)
 
-    @pl.loop(0, slices)
-    def _(m):
-        put([last], m, mine[:4])
+    put_all([last], mine[:4])
 
     y_arrival(5 * line - 6)
 
     for k in range(4):
         x_copy(last, k, 0, w).wait_recv()
 
-    @pl.loop(0, slices)
-    def _(m):
-        put([last], m, mine[4:] + pair, True)
+    put_all([last], mine[4:] + pair, True)
 
     x_copy(last, 4, 0, w).wait_recv()
 
-    @pl.loop(0, slices)
-    def _(m):
-        put([last], m, single, True)
+    put_all([last], single, True)
 
     for j in (line - 3, line - 2):
         c_copy(block_of(j)).wait_recv()
@@ -499,6 +504,7 @@
             pltpu.VMEM((rank // 2 * rows, 2 * rank), jnp.float32),
             pltpu.VMEM((3 * rank // 2, rows * 2 * rank), jnp.bfloat16),
             pltpu.VMEM((chunks, examples, chunk), jnp.bfloat16),
+            pltpu.VMEM((chunks, chunk, examples), jnp.bfloat16),
             pltpu.VMEM((line, chunks, 2, rows, chunk), jnp.bfloat16),
             dma,
             dma((line, 7)),

time: 45.5 us -> 42.8 us (0.941)
  Pallas kernels: 45.3 us -> 42.3 us
    pallas_call x1, Pallas kernels: 43.5 us -> 40.5 us  [scores_of(): pl.pallas_call(functools.partial(score_kernel, line), out_shape=[pltpu.VM...]
where the time goes in v6:
time: 42.8 us; the launch traced here: 42.3 us
  Pallas kernels  42.3 us (99%)
    pallas_call x1, Pallas kernels, scores_of(): pl.pallas_call(functools.partial(score_kernel, line), out_shape=[pltpu.VM...  40.5 us
    pallas_call x1, Pallas kernels, finished(): pl.pallas_call(functools.partial(finish_kernel, line), out_shape=jax.Shap...  1.78 us

profile of v6, /device:TPU:1, one launch (start us, length us, event | category | flops | bytes accessed | tf_op | source)
XLA Modules:
  0.0 42.3 jit_solution(14534666768562215089)
XLA Ops:
  0.0 40.5 %shard_map.64 = (f32[4,128,512]{2,1,0:T(8,128)S(1)}, f32[4,128,1024]{2,1,0:T(8,128)S(1)}, f32[4,128,1024]{2,1,0:T(8,128)S(1)}, bf16[1024,512]{1,0:T(8,128)(2,1)S(1)}) custom-call(bf16[64,4096]{1,0:T(8,128)(2,1)} %bitcast.7, f32[64,64]{1,0:T(8,128)} %bitcast.8, f32[64,64]{1,0:T(8,128)} %bitcast.9, f32[64,64]{1,0:T(8,128)} %bitcast.10, s32[1,1024]{1,0:T(1,128)} %ids_ref.1, ...), custom_call_target="tpu_custom_call" | custom-call | tf_op jit(solution)/shard_map/pallas_call | solution.py:493
  40.5 1.8 %shard_map.65 = f32[4,128,512]{2,1,0:T(8,128)} custom-call(f32[4,128,512]{2,1,0:T(8,128)S(1)} %get-tuple-element.9.total_ref, f32[4,128,1024]{2,1,0:T(8,128)S(1)} %get-tuple-element.10.acc_ref, f32[4,128,1024]{2,1,0:T(8,128)S(1)} %get-tuple-element.11.arrived_ref, bf16[1024,512]{1,0:T(8,128)(2,1)S(1)} %get-tuple-element.12.hot_ref), custom_call_target="tpu_custom_call" | custom-call | tf_op jit(solution)/shard_map/pallas_call | solution.py:554

commit v7 on v6

--- a/solution.py
+++ b/solution.py
@@ -353,11 +353,14 @@
         def _():
             x_copy(b, 4, 0, w).wait_recv()
 
-    def finish(b):
-        c_copy(b).wait_recv()
-        both = jnp.concatenate(split(acc[b] + arrived[b]), axis=0)
-        value = product(both, hot[...])
-        total[b] = value[:2 * rows] + value[2 * rows:]
+    def finish(blocks):
+        for b in blocks:
+            c_copy(b).wait_recv()
+        both = jnp.concatenate([acc[b] + arrived[b] for b in blocks], axis=0)
+        value = product(jnp.concatenate(split(both), axis=0), hot[...])
+        value = value[:both.shape[0]] + value[both.shape[0]:]
+        for i, b in enumerate(blocks):
+            total[b] = value[i * 2 * rows:(i + 1) * 2 * rows]
 
     mine = (2 * side, 2 * side + 1, 4 + side, 6, 7)
     pair = (2 - 2 * side, 3 - 2 * side)
@@ -388,7 +391,7 @@
 
         @pl.when(tick == own_tick + 6)
         def _():
-            finish(zz)
+            finish([zz])
 
         p = (tick - 1) // 12
         step = (tick - 1) % 12
@@ -413,8 +416,7 @@
 
         @pl.when(jnp.logical_and(inside, jnp.logical_and(step == 9, p < line // 2 - 1)))
         def _():
-            finish(one)
-            finish(other)
+            finish([one, other])
 
     @pl.loop(0, ticks)
     def _(tick):
@@ -432,12 +434,15 @@
 
     x_copy(last, 4, 0, w).wait_recv()
 
-    put_all([last], single, True)
-
-    for j in (line - 3, line - 2):
-        c_copy(block_of(j)).wait_recv()
-
-    c_copy(last).start()
+    def c_part(b, n):
+        columns = slice(n * window, (n + 1) * window)
+        return remote(acc.at[b, :, columns], arrived.at[b, :, columns], c_send.at[b], c_recv.at[b], across_c)
+
+    for n in range(slices):
+        put([last], n, single, True)
+        c_part(last, n).start()
+
+    finish([block_of(line - 3), block_of(line - 2)])
     c_copy(last).wait_recv()
 
     def sent(b, count, send):
@@ -521,31 +526,24 @@
 def finish_kernel(line, total_ref, acc_ref, arrived_ref, hot_ref, out_ref, done, sems):
     zz = lax.axis_index("ex") // 2
     rows = total_ref.shape[1]
-    open_blocks = [nth_block(j, zz, line) for j in (line - 3, line - 2, line - 1)]
+    last = nth_block(line - 1, zz, line)
 
     def out_copy(b, source):
         return pltpu.make_async_copy(source, out_ref.at[b], sems.at[b])
 
     @pl.loop(0, line)
     def _(b):
-        ready = jnp.logical_and(b != open_blocks[0], jnp.logical_and(b != open_blocks[1], b != open_blocks[2]))
-
-        @pl.when(ready)
+        @pl.when(b != last)
         def _():
             out_copy(b, total_ref.at[b]).start()
 
-    for base, group in ((0, open_blocks[:2]), (2, open_blocks[2:])):
-        both = jnp.concatenate([acc_ref[b] + arrived_ref[b] for b in group], axis=0)
-        value = product(jnp.concatenate(split(both), axis=0), hot_ref[...])
-        half = both.shape[0]
-        value = value[:half] + value[half:]
-        for i, b in enumerate(group):
-            done[base + i] = value[i * rows:(i + 1) * rows]
-            out_copy(b, done.at[base + i]).start()
+    value = product(jnp.concatenate(split(acc_ref[last] + arrived_ref[last]), axis=0), hot_ref[...])
+    done[...] = value[:rows] + value[rows:]
+    out_copy(last, done).start()
 
     @pl.loop(0, line)
     def _(b):
-        out_copy(b, done.at[0]).wait()
+        out_copy(b, done).wait()
 
 
 def finished(total, acc, arrived, hot):
@@ -557,7 +555,7 @@
         in_specs=[vmem] * 4,
         out_specs=pl.BlockSpec(memory_space=pl.ANY),
         scratch_shapes=[
-            pltpu.VMEM((3, *total.shape[1:]), jnp.float32),
+            pltpu.VMEM(total.shape[1:], jnp.float32),
             pltpu.SemaphoreType.DMA((line,)),
         ],
         compiler_params=pltpu.CompilerParams(vmem_limit_bytes=8 * 1024 * 1024),

time: 42.8 us -> 41.8 us (0.977)
  Pallas kernels: 42.3 us -> 41.6 us
    pallas_call x1, Pallas kernels: 1.78 us -> 1.22 us  [finished(): pl.pallas_call(functools.partial(finish_kernel, line), out_shape=jax.Shap...]
where the time goes in v7:
time: 41.8 us; the launch traced here: 41.6 us
  Pallas kernels  41.6 us (100%)
    pallas_call x1, Pallas kernels, scores_of(): pl.pallas_call(functools.partial(score_kernel, line), out_shape=[pltpu.VM...  40.4 us
    pallas_call x1, Pallas kernels, finished(): pl.pallas_call(functools.partial(finish_kernel, line), out_shape=jax.Shap...  1.22 us

profile of v7, /device:TPU:1, one launch (start us, length us, event | category | flops | bytes accessed | tf_op | source)
XLA Modules:
  0.0 41.6 jit_solution(17892124951938864366)
XLA Ops:
  0.0 40.4 %shard_map.64 = (f32[4,128,512]{2,1,0:T(8,128)S(1)}, f32[4,128,1024]{2,1,0:T(8,128)S(1)}, f32[4,128,1024]{2,1,0:T(8,128)S(1)}, bf16[1024,512]{1,0:T(8,128)(2,1)S(1)}) custom-call(bf16[64,4096]{1,0:T(8,128)(2,1)} %bitcast.7, f32[64,64]{1,0:T(8,128)} %bitcast.8, f32[64,64]{1,0:T(8,128)} %bitcast.9, f32[64,64]{1,0:T(8,128)} %bitcast.10, s32[1,1024]{1,0:T(1,128)} %ids_ref.1, ...), custom_call_target="tpu_custom_call" | custom-call | tf_op jit(solution)/shard_map/pallas_call | solution.py:498
  40.4 1.2 %shard_map.65 = f32[4,128,512]{2,1,0:T(8,128)} custom-call(f32[4,128,512]{2,1,0:T(8,128)S(1)} %get-tuple-element.9.total_ref, f32[4,128,1024]{2,1,0:T(8,128)S(1)} %get-tuple-element.10.acc_ref, f32[4,128,1024]{2,1,0:T(8,128)S(1)} %get-tuple-element.11.arrived_ref, bf16[1024,512]{1,0:T(8,128)(2,1)S(1)} %get-tuple-element.12.hot_ref), custom_call_target="tpu_custom_call" | custom-call | tf_op jit(solution)/shard_map/pallas_call | solution.py:552

commit v8 on v7

--- a/solution.py
+++ b/solution.py
@@ -133,7 +133,7 @@
 def score_kernel(
     line, queries_ref, s_ref, a_ref, eig_ref, ids_ref, train_ref, total, acc, arrived, hot,
     turned, stacked, stored, turned_train, held,
-    load_sem, z_recv, y_recv, x_recv, zr_send, zl_send, y_send, x_send, c_recv, c_send,
+    load_sem, z_recv, y_recv, x_recv, z_send, y_send, x_send, c_send, c_recv,
 ):
     grp = lax.axis_index("grp")
     ex = lax.axis_index("ex")
@@ -176,20 +176,20 @@
             train_ref.at[:, pl.ds(c * chunk, chunk)], stored.at[c], load_sem
         )
 
-    def z_copy(b, k, send, target):
+    def z_copy(b, k, target):
         slot = held.at[b, z_chunk(k), w]
-        return remote(slot, slot, send.at[b], z_recv.at[b, k], target)
+        return remote(slot, slot, z_send, z_recv.at[b, k], target)
 
     def y_copy(b, k, c, column):
         slot = held.at[b, c, column]
-        return remote(slot, slot, y_send.at[b], y_recv.at[b, k], across_y)
+        return remote(slot, slot, y_send, y_recv.at[b, k], across_y)
 
     def x_copy(b, k, c, column):
         slot = held.at[b, c, column]
-        return remote(slot, slot, x_send.at[b], x_recv.at[b, k], across_x)
+        return remote(slot, slot, x_send, x_recv.at[b, k], across_x)
 
     def c_copy(b):
-        return remote(acc.at[b], arrived.at[b], c_send.at[b], c_recv.at[b], across_c)
+        return remote(acc.at[b], arrived.at[b], c_send, c_recv.at[b], across_c)
 
     def block_of(j):
         return nth_block(j, zz, line)
@@ -224,11 +224,11 @@
     def send_z(k):
         @pl.when(has_right)
         def _():
-            z_copy(zz, k, zr_send, right).start()
+            z_copy(zz, k, right).start()
 
         @pl.when(has_left)
         def _():
-            z_copy(zz, k, zl_send, left).start()
+            z_copy(zz, k, left).start()
 
     @pl.loop(0, 6)
     def _(k):
@@ -254,15 +254,15 @@
         hot[tile * 128:(tile + 1) * 128, :] = jnp.where(row == wanted, 1.0, 0.0).astype(jnp.bfloat16)
 
     def z_arrival(b, k, from_left, near):
-        z_copy(b, k, zr_send, right).wait_recv()
+        z_copy(b, k, right).wait_recv()
         if from_left:
             @pl.when(has_right)
             def _():
-                z_copy(b, k, zr_send, right).start()
+                z_copy(b, k, right).start()
         else:
             @pl.when(has_left)
             def _():
-                z_copy(b, k, zl_send, left).start()
+                z_copy(b, k, left).start()
 
         @pl.when(k < 5)
         def _():
@@ -343,7 +343,7 @@
 
         @pl.when(near)
         def _():
-            z_copy(b, 6, zr_send, right).wait_recv()
+            z_copy(b, 6, right).wait_recv()
 
         @pl.when(jnp.logical_not(near))
         def _():
@@ -436,55 +436,32 @@
 
     def c_part(b, n):
         columns = slice(n * window, (n + 1) * window)
-        return remote(acc.at[b, :, columns], arrived.at[b, :, columns], c_send.at[b], c_recv.at[b], across_c)
+        return remote(acc.at[b, :, columns], arrived.at[b, :, columns], c_send, c_recv.at[b], across_c)
 
     for n in range(slices):
         put([last], n, single, True)
         c_part(last, n).start()
 
     finish([block_of(line - 3), block_of(line - 2)])
+    def sent(count, send):
+        span = train_ref.at[pl.ds(0, count * rows // 2), pl.ds(0, 2 * chunk)]
+        remote(span, span, send, c_recv.at[0], across_c).wait_send()
+
+    at_end = both_ways == 0
+
+    @pl.when(at_end)
+    def _():
+        sent(7, z_send)
+        sent(5 * line - 2, x_send)
+
+    @pl.when(jnp.logical_not(at_end))
+    def _():
+        sent(6 * line + 8, z_send)
+        sent(5 * line - 3, x_send)
+
+    sent(5 * line - 1, y_send)
+    remote(acc, arrived, c_send, c_recv.at[0], across_c).wait_send()
     c_copy(last).wait_recv()
-
-    def sent(b, count, send):
-        span = held.at[b, pl.ds(0, count), w]
-        remote(span, span, send.at[b], z_recv.at[b, 0], across_y).wait_send()
-
-    @pl.loop(0, line)
-    def _(b):
-        @pl.when(jnp.logical_and(has_right, b < zz))
-        def _():
-            sent(b, 6, zr_send)
-
-        @pl.when(jnp.logical_and(has_left, b > zz))
-        def _():
-            sent(b, 6, zl_send)
-
-        @pl.when(b == zz)
-        def _():
-            @pl.when(has_right)
-            def _():
-                sent(b, 7, zr_send)
-
-            @pl.when(has_left)
-            def _():
-                sent(b, 7, zl_send)
-
-            sent(b, 4, y_send)
-            sent(b, 4, x_send)
-
-        @pl.when(b != zz)
-        def _():
-            sent(b, 5, y_send)
-
-            @pl.when(jnp.abs(b - zz) == 1)
-            def _():
-                sent(b, 4, x_send)
-
-            @pl.when(jnp.abs(b - zz) != 1)
-            def _():
-                sent(b, 5, x_send)
-
-        c_copy(b).wait_send()
 
 
 def scores_of(queries, basis_s, basis_a, eigvals, ids, train, devices):
@@ -515,7 +492,8 @@
             dma((line, 7)),
             dma((line, 5)),
             dma((line, 5)),
-            *[dma((line,)) for _ in range(6)],
+            *[dma] * 4,
+            dma((line,)),
         ],
         compiler_params=pltpu.CompilerParams(
             collective_id=0, has_side_effects=True, vmem_limit_bytes=52 * 1024 * 1024

time: 41.8 us -> 41.6 us (level)
  no operation moved by 1% of the time
where the time goes in v8:
time: 41.6 us; the launch traced here: 41.4 us
  Pallas kernels  41.4 us (100%)
    pallas_call x1, Pallas kernels, scores_of(): pl.pallas_call(functools.partial(score_kernel, line), out_shape=[pltpu.VM...  40.2 us
    pallas_call x1, Pallas kernels, finished(): pl.pallas_call(functools.partial(finish_kernel, line), out_shape=jax.Shap...  1.22 us

profile of v8, /device:TPU:1, one launch (start us, length us, event | category | flops | bytes accessed | tf_op | source)
XLA Modules:
  0.0 41.4 jit_solution(6866723240719354480)
XLA Ops:
  0.0 40.2 %shard_map.64 = (f32[4,128,512]{2,1,0:T(8,128)S(1)}, f32[4,128,1024]{2,1,0:T(8,128)S(1)}, f32[4,128,1024]{2,1,0:T(8,128)S(1)}, bf16[1024,512]{1,0:T(8,128)(2,1)S(1)}) custom-call(bf16[64,4096]{1,0:T(8,128)(2,1)} %bitcast.7, f32[64,64]{1,0:T(8,128)} %bitcast.8, f32[64,64]{1,0:T(8,128)} %bitcast.9, f32[64,64]{1,0:T(8,128)} %bitcast.10, s32[1,1024]{1,0:T(1,128)} %ids_ref.1, ...), custom_call_target="tpu_custom_call" | custom-call | tf_op jit(solution)/shard_map/pallas_call | solution.py:475
  40.2 1.2 %shard_map.65 = f32[4,128,512]{2,1,0:T(8,128)} custom-call(f32[4,128,512]{2,1,0:T(8,128)S(1)} %get-tuple-element.9.total_ref, f32[4,128,1024]{2,1,0:T(8,128)S(1)} %get-tuple-element.10.acc_ref, f32[4,128,1024]{2,1,0:T(8,128)S(1)} %get-tuple-element.11.arrived_ref, bf16[1024,512]{1,0:T(8,128)(2,1)S(1)} %get-tuple-element.12.hot_ref), custom_call_target="tpu_custom_call" | custom-call | tf_op jit(solution)/shard_map/pallas_call | solution.py:530
